TPU v7x, 32 devices: a whole 2x2x4 slice. The times are simulated.
32 devices in a mesh: dp: 8 (over z, x), tensor: 4 (over y, core).
Axes of the slice: x: 2, y: 2, z: 4, core: 2. Of those that a mesh axis runs over, the one named last changes fastest.
Arguments:
- block_input: float32 [4096, 1024], P(('dp', 'tensor')), may hold values from -6 to 6
- seq_begin: int32 [4096], P('dp'), may hold values from 0 to 511, as said below
- group_fill: int32 [8], P('dp'), may hold values from 256 to 512, as said below
- attention_norm_gain: float32 [1024], P(('dp', 'tensor')), may hold values from 0.1 to 1.9
- attention_norm_bias: float32 [1024], P(('dp', 'tensor')), may hold values from -3 to 3
- qkv_weight: bfloat16 [1024, 3072], P('dp', 'tensor'), may hold values from -0.1875 to 0.1875
- qv_bias: bfloat16 [2048], P(('tensor', 'dp')), may hold values from -3 to 3
- dense_weight: bfloat16 [1024, 1024], P(('tensor', 'dp')), may hold values from -0.5 to 0.5
- dense_bias: float32 [1024], P(('dp', 'tensor')), may hold values from -3 to 3
- feedforward_norm_gain: float32 [1024], P(('dp', 'tensor')), may hold values from 0.1 to 1.9
- feedforward_norm_bias: float32 [1024], P(('dp', 'tensor')), may hold values from -3 to 3
- up_weight: bfloat16 [1024, 4096], P('dp', 'tensor'), may hold values from -0.1875 to 0.1875
- up_bias: bfloat16 [4096], P(('tensor', 'dp')), may hold values from -3 to 3
- down_weight: bfloat16 [4096, 1024], P(('tensor', 'dp')), may hold values from -0.09375 to 0.09375
- down_bias: float32 [1024], P(('dp', 'tensor')), may hold values from -3 to 3
- out_grad: float32 [4096, 1024], P(('dp', 'tensor')), may hold values from -6 to 6
Outputs:
- block_out: float32 [4096, 1024], P(('dp', 'tensor'))
- block_input_gradient: float32 [4096, 1024], P(('dp', 'tensor'))
- attention_gain_gradient: float32 [1024], P(('dp', 'tensor'))
- attn_bias_grad: float32 [1024], P(('dp', 'tensor'))
- qkv_weight_grad: float32 [1024, 3072], P('dp', 'tensor')
- qv_bias_grad: float32 [2048], P(('tensor', 'dp'))
- dense_weight_grad: float32 [1024, 1024], P(('tensor', 'dp'))
- dense_bias_grad: float32 [1024], P(('dp', 'tensor'))
- feedforward_gain_gradient: float32 [1024], P(('dp', 'tensor'))
- mlp_bias_grad: float32 [1024], P(('dp', 'tensor'))
- up_weight_grad: float32 [1024, 4096], P('dp', 'tensor')
- up_bias_grad: float32 [4096], P(('tensor', 'dp'))
- down_weight_grad: float32 [4096, 1024], P(('tensor', 'dp'))
- down_bias_grad: float32 [1024], P(('dp', 'tensor'))
Inputs may be any that keep to these rules, and one draw needn't show every extreme that they name: For row i of a group, seq_begin is the row of the same group where the sequence of row i starts, at most i; rows at or beyond the group's fill have seq_begin equal to their own row. One group in each draw holds a single sequence of 512 rows. `group_fill`: one group in each draw is full.
All inputs are finite; a program needn't handle non-finite values.
Results may differ from a plain program's by a relative error of at most 0.018.
Values may be sent and summed in bfloat16 or wider, within the bound.
A program may use at most 128 MiB of HBM per device.

v0:
```python
import math

import jax
import jax.numpy as jnp
from jax import lax
from jax.sharding import PartitionSpec as P

D = 1024
HEADS = 16


EPSILON = 1e-05
MASKED_SCORE = -1e30
CONTRACT_ROWS = (((0,), (0,)), ((), ()))
CONTRACT_COLS = (((1,), (1,)), ((), ()))


def layer_normalize(hidden_row_count, norm_gain, norm_shift):
    row_mean = jnp.mean(hidden_row_count, axis=-1, keepdims=True)
    centred = hidden_row_count - row_mean
    inv_std = lax.rsqrt(jnp.mean(centred * centred, axis=-1, keepdims=True) + EPSILON)
    normed = centred * inv_std
    return (normed * norm_gain + norm_shift, normed, inv_std)


def norm_backward_step(upstream, norm_gain, normed, inv_std):
    scaled = upstream * norm_gain
    return inv_std * (
        scaled
        - jnp.mean(scaled, axis=-1, keepdims=True)
        - normed * jnp.mean(scaled * normed, axis=-1, keepdims=True)
    )


def gelu_tanh(values_in):
    return jax.nn.gelu(values_in, approximate=True)


def head_slopes(first_head, head_count):
    heads_idx = first_head + jnp.arange(head_count).astype(jnp.float32)
    return jnp.exp2(-8.0 * (heads_idx + 1.0) / HEADS)


def masked_scores(query_blk, key_all, slopes, begin_blk):
    row_count = query_blk.shape[0]
    key_count = key_all.shape[0]
    query_pos = jnp.arange(row_count, dtype=jnp.int32)
    key_pos = jnp.arange(key_count, dtype=jnp.int32)
    score_scale = 1.0 / math.sqrt(query_blk.shape[-1])
    logits = (
        jnp.einsum("qhd,khd->hqk", query_blk, key_all, preferred_element_type=jnp.float32)
        * score_scale
    )
    offset = (key_pos[None, :] - query_pos[:, None]).astype(jnp.float32)
    logits = logits + slopes[:, None, None] * offset[None, :, :]
    allowed = (key_pos[None, :] >= begin_blk[:, None]) & (key_pos[None, :] <= query_pos[:, None])
    return jnp.where(allowed[None, :, :], logits, MASKED_SCORE)


def attention_forward(queries, key_all, values, slopes, begins):
    scores = masked_scores(queries, key_all, slopes, begins)
    row_top = jnp.max(scores, axis=-1)
    log_total = row_top + jnp.log(jnp.sum(jnp.exp(scores - row_top[..., None]), axis=-1))
    attn_probs = jnp.exp(scores - log_total[..., None]).astype(jnp.bfloat16)
    pieces = jnp.einsum(
        "hqk,khd->qhd", attn_probs, values, preferred_element_type=jnp.float32
    ).astype(jnp.bfloat16)
    return (pieces, log_total)


def attention_backward(queries, key_all, values, slopes, begins, log_total, context, context_grad):
    total_rows = queries.shape[0]
    block_rows = min(512, total_rows)
    score_scale = 1.0 / math.sqrt(queries.shape[-1])
    scores = masked_scores(queries, key_all, slopes, begins)
    attn_probs = jnp.exp(scores - log_total[:, 0:block_rows, None])
    row_delta = jnp.sum(context_grad.astype(jnp.float32) * context.astype(jnp.float32), axis=-1)
    value_grad = jnp.einsum(
        "hqk,qhd->khd",
        attn_probs.astype(jnp.bfloat16),
        context_grad,
        preferred_element_type=jnp.float32,
    )
    prob_grad = jnp.einsum("qhd,khd->hqk", context_grad, values, preferred_element_type=jnp.float32)
    score_grad = (attn_probs * (prob_grad - jnp.transpose(row_delta)[:, :, None])).astype(
        jnp.bfloat16
    )
    query_parts = (
        jnp.einsum("hqk,khd->qhd", score_grad, key_all, preferred_element_type=jnp.float32)
        * score_scale
    )
    key_grad = (
        jnp.einsum("hqk,qhd->khd", score_grad, queries, preferred_element_type=jnp.float32)
        * score_scale
    )
    return jnp.stack([query_parts, key_grad, value_grad], axis=2).astype(jnp.bfloat16)


def per_device(
    block_input,
    seq_begin,
    group_fill,
    attention_norm_gain,
    attention_norm_bias,
    qkv_weight,
    qv_bias,
    dense_weight,
    dense_bias,
    feedforward_norm_gain,
    feedforward_norm_bias,
    up_weight,
    up_bias,
    down_weight,
    down_bias,
    out_grad,
):
    vectors = (
        lax.all_gather(attention_norm_gain, ("dp", "tensor"), axis=0, tiled=True),
        lax.all_gather(attention_norm_bias, ("dp", "tensor"), axis=0, tiled=True),
        lax.all_gather(dense_bias, ("dp", "tensor"), axis=0, tiled=True),
        lax.all_gather(feedforward_norm_gain, ("dp", "tensor"), axis=0, tiled=True),
        lax.all_gather(feedforward_norm_bias, ("dp", "tensor"), axis=0, tiled=True),
        lax.all_gather(down_bias, ("dp", "tensor"), axis=0, tiled=True),
    )
    first_gain, first_shift, dense_shift, second_gain, second_shift, down_shift = vectors
    gathered = (
        lax.all_gather(qkv_weight, "dp", axis=0, tiled=True),
        lax.all_gather(qv_bias, "dp", axis=0, tiled=True),
        lax.all_gather(dense_weight, "dp", axis=0, tiled=True),
        lax.all_gather(up_weight, "dp", axis=0, tiled=True),
        lax.all_gather(up_bias, "dp", axis=0, tiled=True),
        lax.all_gather(down_weight, "dp", axis=0, tiled=True),
    )
    qkv_full, qv_full, dense_full, up_full, up_shift, down_full = gathered
    head_dim = D // HEADS
    own_rows = block_input.shape[0]
    group_rows = seq_begin.shape[0]
    local_heads = qkv_full.shape[1] // (3 * head_dim)
    tensor_index = lax.axis_index("tensor")
    row_ids = tensor_index * own_rows + jnp.arange(own_rows, dtype=jnp.int32)
    live_rows = (row_ids < group_fill[0]).astype(jnp.float32)[:, None]
    slopes = head_slopes((tensor_index * local_heads).astype(jnp.float32), local_heads)
    normalized_input, first_standardized, first_inverse_deviation = layer_normalize(
        block_input, first_gain, first_shift
    )
    attn_in = lax.all_gather(normalized_input.astype(jnp.bfloat16), "tensor", axis=0, tiled=True)
    projected = jnp.dot(attn_in, qkv_full, preferred_element_type=jnp.float32).reshape(
        group_rows, local_heads, 3, head_dim
    )
    bias_pair = qv_full.astype(jnp.float32).reshape(local_heads, 2, head_dim)
    bias_full = jnp.stack(
        [bias_pair[:, 0], jnp.zeros_like(bias_pair[:, 0]), bias_pair[:, 1]], axis=1
    )
    qkv_low = (projected + bias_full).astype(jnp.bfloat16)
    queries = qkv_low[:, :, 0]
    key_all = qkv_low[:, :, 1]
    values = qkv_low[:, :, 2]
    context, log_total = attention_forward(queries, key_all, values, slopes, seq_begin)
    context_flat = context.reshape(group_rows, local_heads * head_dim)
    attn_part = jnp.dot(context_flat, dense_full, preferred_element_type=jnp.float32)
    attn_out = lax.psum_scatter(
        attn_part.astype(jnp.bfloat16), "tensor", scatter_dimension=0, tiled=True
    ).astype(jnp.float32)
    residual_middle = block_input + attn_out + dense_shift
    normalized_middle, second_standardized, second_inverse_deviation = layer_normalize(
        residual_middle, second_gain, second_shift
    )
    mlp_in = lax.all_gather(normalized_middle.astype(jnp.bfloat16), "tensor", axis=0, tiled=True)
    pre_act = jnp.dot(mlp_in, up_full, preferred_element_type=jnp.float32) + up_shift.astype(
        jnp.float32
    )
    act_value, act_back = jax.vjp(gelu_tanh, pre_act)
    activated = act_value.astype(jnp.bfloat16)
    mlp_part = jnp.dot(activated, down_full, preferred_element_type=jnp.float32)
    mlp_out = lax.psum_scatter(
        mlp_part.astype(jnp.bfloat16), "tensor", scatter_dimension=0, tiled=True
    ).astype(jnp.float32)
    block_out = residual_middle + mlp_out + down_shift
    running_gradient = out_grad * live_rows
    down_shift_grad = jnp.sum(running_gradient, axis=0)
    out_low = lax.all_gather(running_gradient.astype(jnp.bfloat16), "tensor", axis=0, tiled=True)
    qkv_back, dense_back, up_back, down_back = (
        lax.all_gather(qkv_weight, "dp", axis=0, tiled=True),
        lax.all_gather(dense_weight, "dp", axis=0, tiled=True),
        lax.all_gather(up_weight, "dp", axis=0, tiled=True),
        lax.all_gather(down_weight, "dp", axis=0, tiled=True),
    )
    down_grad = lax.dot_general(
        activated, out_low, CONTRACT_ROWS, preferred_element_type=jnp.float32
    )
    act_grad = lax.dot_general(
        out_low, down_back, CONTRACT_COLS, preferred_element_type=jnp.float32
    )
    pre_grad = act_back(act_grad)[0].astype(jnp.bfloat16)
    up_grad = lax.dot_general(mlp_in, pre_grad, CONTRACT_ROWS, preferred_element_type=jnp.float32)
    up_shift_grad = jnp.sum(pre_grad.astype(jnp.float32), axis=0)
    mlp_in_part = lax.dot_general(
        pre_grad, up_back, CONTRACT_COLS, preferred_element_type=jnp.float32
    )
    feedforward_input_gradient = lax.psum_scatter(
        mlp_in_part.astype(jnp.bfloat16), "tensor", scatter_dimension=0, tiled=True
    ).astype(jnp.float32)
    second_gain_gradient = jnp.sum(feedforward_input_gradient * second_standardized, axis=0)
    shift_two_grad = jnp.sum(feedforward_input_gradient, axis=0)
    residual_middle_gradient = running_gradient + norm_backward_step(
        feedforward_input_gradient, second_gain, second_standardized, second_inverse_deviation
    )
    dense_shift_grad = jnp.sum(residual_middle_gradient, axis=0)
    middle_low = lax.all_gather(
        residual_middle_gradient.astype(jnp.bfloat16), "tensor", axis=0, tiled=True
    )
    dense_grad = lax.dot_general(
        context_flat, middle_low, CONTRACT_ROWS, preferred_element_type=jnp.float32
    )
    context_grad = lax.dot_general(
        middle_low, dense_back, CONTRACT_COLS, preferred_element_type=jnp.float32
    )
    context_grad = context_grad.astype(jnp.bfloat16).reshape(group_rows, local_heads, head_dim)
    qkv_grad = attention_backward(
        queries, key_all, values, slopes, seq_begin, log_total, context, context_grad
    )
    qkv_grad_flat = qkv_grad.reshape(group_rows, 3 * local_heads * head_dim)
    qkv_grad_sum = lax.dot_general(
        attn_in, qkv_grad_flat, CONTRACT_ROWS, preferred_element_type=jnp.float32
    )
    summed = jnp.sum(qkv_grad.astype(jnp.float32), axis=0)
    qv_grad = jnp.stack([summed[:, 0], summed[:, 2]], axis=1).reshape(2 * local_heads * head_dim)
    attn_in_part = lax.dot_general(
        qkv_grad_flat, qkv_back, CONTRACT_COLS, preferred_element_type=jnp.float32
    )
    attention_input_gradient = lax.psum_scatter(
        attn_in_part.astype(jnp.bfloat16), "tensor", scatter_dimension=0, tiled=True
    ).astype(jnp.float32)
    first_gain_gradient = jnp.sum(attention_input_gradient * first_standardized, axis=0)
    shift_one_grad = jnp.sum(attention_input_gradient, axis=0)
    block_input_gradient = residual_middle_gradient + norm_backward_step(
        attention_input_gradient, first_gain, first_standardized, first_inverse_deviation
    )
    weight_parts = (
        lax.psum_scatter(qkv_grad_sum, "dp", scatter_dimension=0, tiled=True),
        lax.psum_scatter(qv_grad, "dp", scatter_dimension=0, tiled=True),
        lax.psum_scatter(dense_grad, "dp", scatter_dimension=0, tiled=True),
        lax.psum_scatter(up_grad, "dp", scatter_dimension=0, tiled=True),
        lax.psum_scatter(up_shift_grad, "dp", scatter_dimension=0, tiled=True),
        lax.psum_scatter(down_grad, "dp", scatter_dimension=0, tiled=True),
    )
    vector_parts = (
        lax.psum_scatter(first_gain_gradient, ("dp", "tensor"), scatter_dimension=0, tiled=True),
        lax.psum_scatter(shift_one_grad, ("dp", "tensor"), scatter_dimension=0, tiled=True),
        lax.psum_scatter(dense_shift_grad, ("dp", "tensor"), scatter_dimension=0, tiled=True),
        lax.psum_scatter(second_gain_gradient, ("dp", "tensor"), scatter_dimension=0, tiled=True),
        lax.psum_scatter(shift_two_grad, ("dp", "tensor"), scatter_dimension=0, tiled=True),
        lax.psum_scatter(down_shift_grad, ("dp", "tensor"), scatter_dimension=0, tiled=True),
    )
    return (
        block_out,
        block_input_gradient,
        vector_parts[0],
        vector_parts[1],
        weight_parts[0],
        weight_parts[1],
        weight_parts[2],
        vector_parts[2],
        vector_parts[3],
        vector_parts[4],
        weight_parts[3],
        weight_parts[4],
        weight_parts[5],
        vector_parts[5],
    )


def solution(mesh):
    return jax.shard_map(
        per_device,
        mesh=mesh,
        in_specs=(
            P(("dp", "tensor"), None),
            P("dp"),
            P("dp"),
            P(("dp", "tensor")),
            P(("dp", "tensor")),
            P("dp", "tensor"),
            P(("tensor", "dp")),
            P(("tensor", "dp"), None),
            P(("dp", "tensor")),
            P(("dp", "tensor")),
            P(("dp", "tensor")),
            P("dp", "tensor"),
            P(("tensor", "dp")),
            P(("tensor", "dp"), None),
            P(("dp", "tensor")),
            P(("dp", "tensor"), None),
        ),
        out_specs=(
            P(("dp", "tensor"), None),
            P(("dp", "tensor"), None),
            P(("dp", "tensor")),
            P(("dp", "tensor")),
            P("dp", "tensor"),
            P(("tensor", "dp")),
            P(("tensor", "dp"), None),
            P(("dp", "tensor")),
            P(("dp", "tensor")),
            P(("dp", "tensor")),
            P("dp", "tensor"),
            P(("tensor", "dp")),
            P(("tensor", "dp"), None),
            P(("dp", "tensor")),
        ),
        check_vma=False,
    )
```

profile of v0, /device:TPU:0, one launch (start us, length us, event | category | flops | bytes accessed | tf_op | source)
XLA Modules:
  0.0 745.9 jit_solution(14437159159798137099)
XLA Ops:
  7.3 1.2 reduce_sum.162
  8.4 1.2 multiply_reduce_fusion.2
  9.7 0.9 dynamic-update-slice.1
  10.6 0.8 dynamic-update-slice
  11.4 0.8 dynamic-update-slice.3
  12.2 0.8 dynamic-update-slice.5
  13.1 0.8 dynamic-update-slice.4
  13.9 42.3 %all-reduce.16 = (f32[1024]{0:T(1024)S(1)}, f32[1024]{0:T(1024)S(1)}, f32[1024]{0:T(1024)S(1)}, f32[1024]{0:T(1024)S(1)}, f32[1024]{0:T(1024)S(1)}) all-reduce(f32[1024]{0:T(1024)S(1)} %dynamic-update-slice.1, f32[1024]{0:T(1024)S(1)} %dynamic-update-slice, ...), channel_id=1, replica_groups=mesh['dp'=8,'tensor'=4] {'dp','tensor'}, use_global_device_ids=true, to_apply=%add.1 | all-reduce | flops 5120 | bytes 40960
  56.2 1.9 add_convert_fusion.1
  58.2 0.7 all-gather.11.cloned.1.call-update
  58.9 0.6 fusion.37
  60.4 21.1 %all-reduce.2 = bf16[512]{0:T(512)(128)(2,1)S(1)} all-reduce(bf16[512]{0:T(512)(128)(2,1)S(1)} %dynamic-update-slice.2), channel_id=1, replica_groups=mesh['dp'=8,'tensor'=4] {'dp'}, use_global_device_ids=true, to_apply=%add.2 | all-reduce | flops 512 | bytes 2048
  82.0 32.6 %all_gather.57 = bf16[256,1024]{1,0:T(8,128)(2,1)S(1)} all-gather(bf16[32,1024]{1,0:T(8,128)(2,1)S(1)} %copy-done.8), channel_id=1, replica_groups=mesh['dp'=8,'tensor'=4] {'dp'}, dimensions={0}, use_global_device_ids=true | all-gather | bytes 589824 | tf_op jit(solution)/shard_map/all_gather | solution.py:129
  114.7 9.1 %all-gather.11.cloned.1.call-done = bf16[1024,768]{1,0:T(8,128)(2,1)} async-done(((bf16[128,768]{1,0:T(8,128)(2,1)}), bf16[1024,768]{1,0:T(8,128)(2,1)}) %all-gather.11.cloned.1.call-update) | async-done | bytes 1572880 | tf_op jit(solution)/shard_map/all_gather | solution.py:127
  123.8 2.7 fusion.39
  126.8 1.3 fusion.38
  128.1 0.6 exponential_reduce_fusion
  128.7 1.4 copy-done
  130.1 0.8 convolution_convert_fusion.5
  130.9 1.4 convolution_convert_fusion.3
  133.0 22.9 %reduce-scatter.9.cloned.1.call-done = bf16[128,1024]{1,0:T(8,128)(2,1)} async-done(((bf16[512,1024]{1,0:T(8,128)(2,1)}), bf16[128,1024]{1,0:T(8,128)(2,1)}) %reduce-scatter.9.cloned.1.call-update) | async-done | bytes 262160 | tf_op jit(solution)/shard_map/reduce_scatter | solution.py:161
  155.9 1.1 fusion.34
  157.2 0.9 add_convert_fusion
  158.8 0.8 multiply_convert_fusion.2
  159.7 0.7 all-gather.17.cloned.1.call-update
  160.5 20.8 %all-gather = bf16[8,1,128]{2,1,0:T(2,128)(2,1)S(1)} all-gather(bf16[1,1,128]{2,1,0:T(2,128)(2,1)S(1)} %bitcast.81), channel_id=1, replica_groups=mesh['dp'=8,'tensor'=4] {'dp'}, dimensions={0}, use_global_device_ids=true | all-gather | bytes 2304 | tf_op jit(solution)/shard_map/all_gather | solution.py:131
  181.3 25.7 %all-gather.15.cloned.1.call-done = bf16[1024,1024]{1,0:T(8,128)(2,1)} async-done(((bf16[128,1024]{1,0:T(8,128)(2,1)}), bf16[1024,1024]{1,0:T(8,128)(2,1)}) %all-gather.15.cloned.1.call-update) | async-done | bytes 2097168 | tf_op jit(solution)/shard_map/all_gather | solution.py:130
  207.0 17.2 %all-gather.13.cloned.1.call-done = bf16[512,1024]{1,0:T(8,128)(2,1)} async-done(((bf16[128,1024]{1,0:T(8,128)(2,1)}), bf16[512,1024]{1,0:T(8,128)(2,1)}) %all-gather.13.cloned.1.call-update) | async-done | bytes 1048592 | tf_op jit(solution)/shard_map/all_gather | solution.py:168
  224.3 4.5 fusion.40
  228.8 14.2 %all-gather.19.cloned.1.call-done = bf16[512,1024]{1,0:T(8,128)(2,1)} async-done(((bf16[128,1024]{1,0:T(8,128)(2,1)}), bf16[512,1024]{1,0:T(8,128)(2,1)}) %all-gather.19.cloned.1.call-update) | async-done | bytes 1048592 | tf_op jit(solution)/shard_map/all_gather | solution.py:181
  243.0 51.2 %all-gather.17.cloned.1.call-done = bf16[1024,1024]{1,0:T(8,128)(2,1)} async-done(((bf16[128,1024]{1,0:T(8,128)(2,1)}), bf16[1024,1024]{1,0:T(8,128)(2,1)}) %all-gather.17.cloned.1.call-update) | async-done | bytes 2097168 | tf_op jit(solution)/shard_map/all_gather | solution.py:132
  294.3 5.2 convert_reduce_fusion
  299.4 1.0 copy-done.7
  300.4 2.3 convolution_convert_fusion.1
  302.7 23.4 %reduce-scatter.13.cloned.1.call-done = bf16[128,1024]{1,0:T(8,128)(2,1)} async-done(((bf16[512,1024]{1,0:T(8,128)(2,1)}), bf16[128,1024]{1,0:T(8,128)(2,1)}) %reduce-scatter.13.cloned.1.call-update) | async-done | bytes 262160 | tf_op jit(solution)/shard_map/reduce_scatter | solution.py:200
  326.2 1.2 fusion.28
  327.4 1.2 fusion.32
  328.6 0.7 convert_element_type.129
  329.5 16.8 %all-gather.21.cloned.1.call-done = bf16[512,1024]{1,0:T(8,128)(2,1)} async-done(((bf16[128,1024]{1,0:T(8,128)(2,1)}), bf16[512,1024]{1,0:T(8,128)(2,1)}) %all-gather.21.cloned.1.call-update) | async-done | bytes 1048592 | tf_op jit(solution)/shard_map/all_gather | solution.py:209
  346.3 1.9 multiply_reduce_fusion
  348.1 3.1 convolution_bitcast_fusion
  351.6 1.0 multiply_convert_fusion
  352.6 0.8 fusion.9
  354.1 1.1 copy-done.13
  355.3 2.0 convolution_convert_fusion
  357.4 4.8 convolution_convert_fusion.2
  362.3 2.7 fusion.42
  365.1 5.0 fusion.43
  370.3 0.9 copy-done.14
  371.3 5.1 fusion.30
  376.5 1.1 copy-done.3
  377.6 2.7 fusion.41
  382.0 21.7 %all-reduce.17 = (f32[512]{0:T(512)S(1)}, f32[1024]{0:T(1024)S(1)}) all-reduce(f32[512]{0:T(512)S(1)} %reshape.168, f32[1024]{0:T(1024)S(1)} %get-tuple-element.36), channel_id=9, replica_groups=mesh['dp'=8,'tensor'=4] {'dp'}, use_global_device_ids=true, to_apply=%region_21.22.clone | all-reduce | flops 1536 | bytes 12288
  403.7 0.6 dynamic-slice.4
  404.9 1.3 fusion.29
  406.1 37.6 %all-reduce.15 = (f32[1024]{0:T(1024)S(1)}, f32[1024]{0:T(1024)S(1)}, f32[1024]{0:T(1024)S(1)}, f32[1024]{0:T(1024)S(1)}, f32[1024]{0:T(1024)S(1)}, /*index=5*/f32[1024]{0:T(1024)S(1)}, f32[1024]{0:T(1024)S(1)}) all-reduce(f32[1024]{0:T(1024)S(1)} %dynamic-update-slice.6, ...), channel_id=1, replica_groups=mesh['dp'=8,'tensor'=4] {'dp','tensor'}, use_global_device_ids=true, to_apply=%add.6 | all-reduce | flops 7168 | bytes 57344
  443.8 0.6 dynamic-slice.1
  445.0 0.6 dynamic-slice.5
  447.3 1.8 add_add_fusion
  449.1 1.0 fusion.22
  450.1 27.6 %reduce-scatter.19.cloned.1.call-done = f32[32,1024]{1,0:T(8,128)} async-done(((f32[256,1024]{1,0:T(8,128)}), f32[32,1024]{1,0:T(8,128)}) %reduce-scatter.19.cloned.1.call-update) | async-done | bytes 131088 | tf_op jit(solution)/shard_map/reduce_scatter | solution.py:242
  477.8 91.6 %reduce-scatter.21.cloned.1.call-done = f32[128,1024]{1,0:T(8,128)} async-done(((f32[1024,1024]{1,0:T(8,128)}), f32[128,1024]{1,0:T(8,128)}) %reduce-scatter.21.cloned.1.call-update) | async-done | bytes 524304 | tf_op jit(solution)/shard_map/reduce_scatter | solution.py:243
  569.3 92.0 %reduce-scatter.23.cloned.1.call-done = f32[128,1024]{1,0:T(8,128)} async-done(((f32[1024,1024]{1,0:T(8,128)}), f32[128,1024]{1,0:T(8,128)}) %reduce-scatter.23.cloned.1.call-update) | async-done | bytes 524304 | tf_op jit(solution)/shard_map/reduce_scatter | solution.py:245
  661.4 78.0 %reduce-scatter.17.cloned.1.call-done = f32[128,768]{1,0:T(8,128)} async-done(((f32[1024,768]{1,0:T(8,128)}), f32[128,768]{1,0:T(8,128)}) %reduce-scatter.17.cloned.1.call-update) | async-done | bytes 393232 | tf_op jit(solution)/shard_map/reduce_scatter | solution.py:240
  (101 shorter events, 7.2 us)
Async XLA Ops:
  7.2 51.8 %copy-start.10 = (u32[32]{0:T(128)S(1)}, u32[32]{0:T(128)}, u32[]{:S(2)}) copy-start(u32[32]{0:T(128)} %constant.61) | copy-start | bytes 388
  7.2 53.0 %copy-start.15 = (bf16[64]{0:T(256)(128)(2,1)S(1)}, bf16[64]{0:T(256)(128)(2,1)}, u32[]{:S(2)}) copy-start(bf16[64]{0:T(256)(128)(2,1)} %param.22) | copy-start | bytes 388
  7.2 74.8 %copy-start.8 = (bf16[32,1024]{1,0:T(8,128)(2,1)S(1)}, bf16[32,1024]{1,0:T(8,128)(2,1)}, u32[]{:S(2)}) copy-start(bf16[32,1024]{1,0:T(8,128)(2,1)} %param.23) | copy-start | bytes 196612
  7.2 107.3 %copy-start.9 = (s32[512]{0:T(512)S(1)}, s32[512]{0:T(512)}, u32[]{:S(2)}) copy-start(s32[512]{0:T(512)} %param.17) | copy-start | bytes 6148
  7.2 107.5 %all-gather.9.cloned.1.call-start = ((), (), s32[]{:S(2)}) async-start(), calls=%async_computation.8 | async-start | bytes 1310720 | tf_op jit(solution)/shard_map/all_gather | solution.py:146
  58.1 65.7 %all-gather.11.cloned.1.call-start = ((), (), s32[]{:S(2)}) async-start(), calls=%async_computation.9 | async-start | bytes 1769472 | tf_op jit(solution)/shard_map/all_gather | solution.py:127
  58.9 97.0 %reduce-scatter.9.cloned.1.call-start = ((), (), s32[]{:S(2)}) async-start(), calls=%async_computation.10 | async-start | bytes 1310720 | tf_op jit(solution)/shard_map/reduce_scatter | solution.py:161
  114.6 16.4 %copy-start.5 = (bf16[256,1024]{1,0:T(8,128)(2,1)}, bf16[256,1024]{1,0:T(8,128)(2,1)S(1)}, u32[]{:S(2)}) copy-start(bf16[256,1024]{1,0:T(8,128)(2,1)S(1)} %all_gather.57) | copy-start | bytes 1572868
  128.1 2.0 copy-start
  130.9 25.0 %copy-start.2 = (f32[128,1024]{1,0:T(8,128)S(1)}, f32[128,1024]{1,0:T(8,128)}, u32[]{:S(2)}) copy-start(f32[128,1024]{1,0:T(8,128)} %param.16) | copy-start | bytes 1572868
  132.4 26.5 %copy-start.4 = (f32[128,1024]{1,0:T(8,128)S(1)}, f32[128,1024]{1,0:T(8,128)}, u32[]{:S(2)}) copy-start(f32[128,1024]{1,0:T(8,128)} %param.31) | copy-start | bytes 1572868
  132.4 74.7 %all-gather.15.cloned.1.call-start = ((), (), s32[]{:S(2)}) async-start(), calls=%async_computation.12 | async-start | bytes 2359296 | tf_op jit(solution)/shard_map/all_gather | solution.py:130
  133.0 91.3 %all-gather.13.cloned.1.call-start = ((), (), s32[]{:S(2)}) async-start(), calls=%async_computation.11 | async-start | bytes 1310720 | tf_op jit(solution)/shard_map/all_gather | solution.py:168
  155.9 4.6 copy-start.11
  158.1 84.9 %all-gather.19.cloned.1.call-start = ((), (), s32[]{:S(2)}) async-start(), calls=%async_computation.15 | async-start | bytes 1310720 | tf_op jit(solution)/shard_map/all_gather | solution.py:181
  159.7 134.6 %all-gather.17.cloned.1.call-start = ((), (), s32[]{:S(2)}) async-start(), calls=%async_computation.13 | async-start | bytes 2359296 | tf_op jit(solution)/shard_map/all_gather | solution.py:132
  160.4 165.8 %reduce-scatter.13.cloned.1.call-start = ((), (), s32[]{:S(2)}) async-start(), calls=%async_computation.16 | async-start | bytes 1310720 | tf_op jit(solution)/shard_map/reduce_scatter | solution.py:200
  294.3 6.1 copy-start.12
  299.4 1.0 copy-start.7
  302.7 43.6 %all-gather.21.cloned.1.call-start = ((), (), s32[]{:S(2)}) async-start(), calls=%async_computation.17 | async-start | bytes 1310720 | tf_op jit(solution)/shard_map/all_gather | solution.py:209
  329.4 75.4 %reduce-scatter.15.cloned.1.call-start = ((), (), s32[]{:S(2)}) async-start(), calls=%async_computation.18 | async-start | bytes 1310720 | tf_op jit(solution)/shard_map/reduce_scatter | solution.py:231
  348.1 3.5 copy-start.1
  353.9 1.4 copy-start.13
  357.3 90.0 %reduce-scatter.11.cloned.1.call-start = ((), (), s32[]{:S(2)}) async-start(), calls=%async_computation.14 | async-start | bytes 1310720 | tf_op jit(solution)/shard_map/reduce_scatter | solution.py:175
  362.2 115.5 %reduce-scatter.19.cloned.1.call-start = ((), (), s32[]{:S(2)}) async-start(), calls=%async_computation.20 | async-start | bytes 1179648 | tf_op jit(solution)/shard_map/reduce_scatter | solution.py:242
  365.0 204.3 %reduce-scatter.21.cloned.1.call-start = ((), (), s32[]{:S(2)}) async-start(), calls=%async_computation.21 | async-start | bytes 4718592 | tf_op jit(solution)/shard_map/reduce_scatter | solution.py:243
  370.0 1.2 copy-start.14
  370.1 291.3 %reduce-scatter.23.cloned.1.call-start = ((), (), s32[]{:S(2)}) async-start(), calls=%async_computation.22 | async-start | bytes 4718592 | tf_op jit(solution)/shard_map/reduce_scatter | solution.py:245
  376.4 1.2 copy-start.3
  376.4 363.0 %reduce-scatter.17.cloned.1.call-start = ((), (), s32[]{:S(2)}) async-start(), calls=%async_computation.19 | async-start | bytes 3538944 | tf_op jit(solution)/shard_map/reduce_scatter | solution.py:240
  380.3 1.3 copy-start.16
  404.9 44.3 %copy-start.6 = (bf16[128,1024]{1,0:T(8,128)(2,1)S(1)}, bf16[128,1024]{1,0:T(8,128)(2,1)}, u32[]{:S(2)}) copy-start(bf16[128,1024]{1,0:T(8,128)(2,1)} %reduce-scatter.15.cloned.1.call-done) | copy-start | bytes 786436
Sparse Core Ops, SparseCore 0:
  58.2 16.5 all-gather.8
  77.0 46.7 all-gather.10
  132.5 23.3 reduce-scatter.8
  157.9 49.1 all-gather.14
  209.0 15.2 all-gather.12
  226.3 16.6 all-gather.18
  245.1 49.0 all-gather.16
  302.8 23.3 reduce-scatter.12
  329.5 16.6 all-gather.20
  357.4 24.7 reduce-scatter.14
  384.8 24.7 reduce-scatter.10
  413.5 64.2 reduce-scatter.18
  482.0 87.3 reduce-scatter.20
  573.4 87.9 reduce-scatter.22
  665.4 73.9 reduce-scatter.16
where the time goes:
time: 747 us; the launch traced here: 746 us
  waiting for transfers between devices  472 us (63%)
  blocking collectives  176 us (24%)
  matrix products  47.9 us (6%)
  between operations  16.9 us (2%)
  local copies, waits for them, and re-layouts  16.2 us (2%)
  other arithmetic  16 us (2%)
    unnamed x4, blocking collectives  123 us
    reduce_scatter x1, waiting for transfers between devices, per_device(): lax.psum_scatter(down_grad, 'dp', scatter_dimension=0, tiled=True)  92 us
    reduce_scatter x1, waiting for transfers between devices, per_device(): lax.psum_scatter(up_grad, 'dp', scatter_dimension=0, tiled=True)  91.6 us
    reduce_scatter x1, waiting for transfers between devices, per_device(): lax.psum_scatter(qkv_grad_sum, 'dp', scatter_dimension=0, tiled=True)  78 us
    all_gather x1, waiting for transfers between devices, per_device(): lax.all_gather(down_weight, 'dp', axis=0, tiled=True)  51.2 us
    all_gather x1, blocking collectives, per_device(): lax.all_gather(dense_weight, 'dp', axis=0, tiled=True)  32.6 us
    reduce_scatter x1, waiting for transfers between devices, per_device(): lax.psum_scatter(dense_grad, 'dp', scatter_dimension=0, tiled=True)  27.6 us
    all_gather x1, waiting for transfers between devices, per_device(): lax.all_gather(up_weight, 'dp', axis=0, tiled=True)  25.7 us
  transfers between devices with their start and end apart: 15, of which 12 were waited for; matrix products, arithmetic and copies ran while one was open for 5% of the time, Pallas kernels for 0%

commit v1 on v0

v1 whole, which is shorter than its diff:
```python
import functools
import math

import jax
import jax.numpy as jnp
from jax import lax
from jax.experimental import pallas as pl
from jax.experimental.pallas import tpu as pltpu
from jax.sharding import PartitionSpec as P

D = 1024
HEADS = 16


EPSILON = 1e-05
MASKED_SCORE = -1e30
CONTRACT_ROWS = (((0,), (0,)), ((), ()))
CONTRACT_COLS = (((1,), (1,)), ((), ()))


def layer_normalize(hidden_row_count, norm_gain, norm_shift):
    row_mean = jnp.mean(hidden_row_count, axis=-1, keepdims=True)
    centred = hidden_row_count - row_mean
    inv_std = lax.rsqrt(jnp.mean(centred * centred, axis=-1, keepdims=True) + EPSILON)
    normed = centred * inv_std
    return (normed * norm_gain + norm_shift, normed, inv_std)


def norm_backward_step(upstream, norm_gain, normed, inv_std):
    scaled = upstream * norm_gain
    return inv_std * (
        scaled
        - jnp.mean(scaled, axis=-1, keepdims=True)
        - normed * jnp.mean(scaled * normed, axis=-1, keepdims=True)
    )


def gelu_tanh(values_in):
    return jax.nn.gelu(values_in, approximate=True)


def head_slopes(first_head, head_count):
    heads_idx = first_head + jnp.arange(head_count).astype(jnp.float32)
    return jnp.exp2(-8.0 * (heads_idx + 1.0) / HEADS)


def masked_scores(query_blk, key_all, slopes, begin_blk):
    row_count = query_blk.shape[0]
    key_count = key_all.shape[0]
    query_pos = jnp.arange(row_count, dtype=jnp.int32)
    key_pos = jnp.arange(key_count, dtype=jnp.int32)
    score_scale = 1.0 / math.sqrt(query_blk.shape[-1])
    logits = (
        jnp.einsum("qhd,khd->hqk", query_blk, key_all, preferred_element_type=jnp.float32)
        * score_scale
    )
    offset = (key_pos[None, :] - query_pos[:, None]).astype(jnp.float32)
    logits = logits + slopes[:, None, None] * offset[None, :, :]
    allowed = (key_pos[None, :] >= begin_blk[:, None]) & (key_pos[None, :] <= query_pos[:, None])
    return jnp.where(allowed[None, :, :], logits, MASKED_SCORE)


def attention_forward(queries, key_all, values, slopes, begins):
    scores = masked_scores(queries, key_all, slopes, begins)
    row_top = jnp.max(scores, axis=-1)
    log_total = row_top + jnp.log(jnp.sum(jnp.exp(scores - row_top[..., None]), axis=-1))
    attn_probs = jnp.exp(scores - log_total[..., None]).astype(jnp.bfloat16)
    pieces = jnp.einsum(
        "hqk,khd->qhd", attn_probs, values, preferred_element_type=jnp.float32
    ).astype(jnp.bfloat16)
    return (pieces, log_total)


def attention_backward(queries, key_all, values, slopes, begins, log_total, context, context_grad):
    total_rows = queries.shape[0]
    block_rows = min(512, total_rows)
    score_scale = 1.0 / math.sqrt(queries.shape[-1])
    scores = masked_scores(queries, key_all, slopes, begins)
    attn_probs = jnp.exp(scores - log_total[:, 0:block_rows, None])
    row_delta = jnp.sum(context_grad.astype(jnp.float32) * context.astype(jnp.float32), axis=-1)
    value_grad = jnp.einsum(
        "hqk,qhd->khd",
        attn_probs.astype(jnp.bfloat16),
        context_grad,
        preferred_element_type=jnp.float32,
    )
    prob_grad = jnp.einsum("qhd,khd->hqk", context_grad, values, preferred_element_type=jnp.float32)
    score_grad = (attn_probs * (prob_grad - jnp.transpose(row_delta)[:, :, None])).astype(
        jnp.bfloat16
    )
    query_parts = (
        jnp.einsum("hqk,khd->qhd", score_grad, key_all, preferred_element_type=jnp.float32)
        * score_scale
    )
    key_grad = (
        jnp.einsum("hqk,qhd->khd", score_grad, queries, preferred_element_type=jnp.float32)
        * score_scale
    )
    return jnp.stack([query_parts, key_grad, value_grad], axis=2).astype(jnp.bfloat16)

MESH = pl.DeviceIdType.MESH
VECTOR_ROWS = 8
BF16 = jnp.bfloat16
F32 = jnp.float32


def place():
    return lax.axis_index("dp"), lax.axis_index("tensor")


def tensor_peers(t):
    h, c = t // 2, t % 2
    core = h * 2 + (1 - c)
    across = (1 - h) * 2 + c
    diagonal = (1 - h) * 2 + (1 - c)
    return core, across, diagonal


def enter(dp_count):
    d, t = place()
    barrier = pltpu.get_barrier_semaphore()
    for j in range(1, 4):
        pl.semaphore_signal(
            barrier, inc=1, device_id=(d, lax.rem(t + j, 4)), device_id_type=MESH
        )
    if dp_count == 1:
        pl.semaphore_wait(barrier, 3)
        return

    def greet(j, carry):
        pl.semaphore_signal(
            barrier, inc=1, device_id=(lax.rem(d + j, dp_count), t), device_id_type=MESH
        )
        return carry

    lax.fori_loop(1, dp_count, greet, 0)
    pl.semaphore_wait(barrier, 3 + dp_count - 1)


def remote(src, dst, send, recv, d, t):
    return pltpu.make_async_remote_copy(
        src_ref=src, dst_ref=dst, send_sem=send, recv_sem=recv, device_id=(d, t), device_id_type=MESH
    )


class VectorSum:
    def __init__(self, dp_count, dbuf, tbuf, dsend, drecv, tsend, trecv):
        self.dp_count = dp_count
        self.dbuf, self.tbuf = dbuf, tbuf
        self.dsend, self.drecv, self.tsend, self.trecv = dsend, drecv, tsend, trecv

    @staticmethod
    def scratch(dp_count, width):
        return [
            pltpu.VMEM((dp_count, VECTOR_ROWS, width), F32),
            pltpu.VMEM((4, VECTOR_ROWS, width), F32),
            pltpu.SemaphoreType.DMA((dp_count,)),
            pltpu.SemaphoreType.DMA((dp_count,)),
            pltpu.SemaphoreType.DMA((4,)),
            pltpu.SemaphoreType.DMA((4,)),
        ]

    def dcopy(self, j):
        d, t = place()
        return remote(
            self.dbuf.at[0], self.dbuf.at[j], self.dsend.at[j], self.drecv.at[j],
            lax.rem(d + j, self.dp_count), t,
        )

    def tcopy(self, j):
        d, t = place()
        return remote(
            self.tbuf.at[0], self.tbuf.at[j], self.tsend.at[j], self.trecv.at[j],
            d, lax.rem(t + j, 4),
        )

    def start(self, value):
        self.dbuf[0] = value

        def go(j, carry):
            self.dcopy(j).start()
            return carry

        lax.fori_loop(1, self.dp_count, go, 0)

    def middle(self):
        def wait(j, carry):
            self.dcopy(j).wait()
            return carry

        lax.fori_loop(1, self.dp_count, wait, 0)
        self.tbuf[0] = jnp.sum(self.dbuf[...], axis=0)
        for j in range(1, 4):
            self.tcopy(j).start()

    def finish(self):
        for j in range(1, 4):
            self.tcopy(j).wait()
        own = self.tbuf[0]
        total = own + self.tbuf[1] + self.tbuf[2] + self.tbuf[3]
        row = lax.broadcasted_iota(jnp.int32, own.shape, 0)
        return jnp.where(row < 6, total, own)


class TensorGather:
    def __init__(self, buf, send, recv):
        self.buf, self.send, self.recv = buf, send, recv
        d, t = place()
        core, across, diagonal = tensor_peers(t)
        half = buf.shape[1] // 2
        part = [pl.ds(k * half, half) for k in range(2)]
        at = lambda s, k: buf.at[s, part[k]]
        self.to_across = [
            remote(at(t, k), at(t, k), send.at[k], recv.at[k], d, across) for k in range(2)
        ]
        self.to_core = [
            remote(at(t, k), at(t, k), send.at[2 + k], recv.at[2 + k], d, core) for k in range(2)
        ]
        self.relay = [
            remote(at(across, k), at(across, k), send.at[4 + k], recv.at[4 + k], d, core)
            for k in range(2)
        ]

    @staticmethod
    def scratch():
        return [pltpu.SemaphoreType.DMA((6,)), pltpu.SemaphoreType.DMA((6,))]

    def start(self, value):
        _, t = place()
        self.buf[t] = value
        for c in self.to_across + self.to_core:
            c.start()

    def forward(self):
        for k in range(2):
            self.to_across[k].wait_recv()
            self.relay[k].start()

    def finish(self):
        for c in self.to_across:
            c.wait_send()
        for c in self.to_core + self.relay:
            c.wait()


class TensorScatter:
    def __init__(self, part, near, far, out, send, recv):
        self.part, self.near, self.far, self.out = part, near, far, out
        d, t = place()
        core, across, diagonal = tensor_peers(t)
        half = part.shape[1] // 2
        self.rows = [pl.ds(k * half, half) for k in range(2)]
        r = self.rows
        self.first = [
            remote(part.at[diagonal, r[k]], near.at[1, r[k]], send.at[k], recv.at[k], d, core)
            for k in range(2)
        ]
        self.own = [
            remote(part.at[core, r[k]], near.at[0, r[k]], send.at[2 + k], recv.at[2 + k], d, core)
            for k in range(2)
        ]
        self.second = [
            remote(out.at[r[k]], far.at[r[k]], send.at[4 + k], recv.at[4 + k], d, across)
            for k in range(2)
        ]

    @staticmethod
    def scratch(rows, width):
        return [
            pltpu.VMEM((2, rows, width), BF16),
            pltpu.VMEM((rows, width), BF16),
            pltpu.VMEM((rows, width), BF16),
            pltpu.SemaphoreType.DMA((6,)),
            pltpu.SemaphoreType.DMA((6,)),
        ]

    def start(self):
        for c in self.first + self.own:
            c.start()

    def middle(self):
        _, t = place()
        _, across, _ = tensor_peers(t)
        for k in range(2):
            self.first[k].wait_recv()
            r = self.rows[k]
            self.out[r] = (
                self.part[across, r].astype(F32) + self.near[1, r].astype(F32)
            ).astype(BF16)
            self.second[k].start()

    def finish(self):
        _, t = place()
        for c in self.first:
            c.wait_send()
        for c in self.own + self.second:
            c.wait()
        return (
            self.part[t].astype(F32) + self.near[0].astype(F32) + self.far[...].astype(F32)
        )


def gather_kernel(dp_count, *refs):
    (vec_ref, x_ref, og_ref, w0, w1, w2, w3,
     vec_out, attn_in, out_low, o0, o1, o2, o3,
     *scratch) = refs
    weights = list(zip((w0, w1, w2, w3), (o0, o1, o2, o3)))
    zsend, xsend, wrecv, lsem = scratch[:4]
    vsum = VectorSum(dp_count, *scratch[4:10])
    d, t = place()
    line, b = d // 2, d % 2
    line_count = dp_count // 2
    enter(dp_count)
    vsum.start(vec_ref[...])
    gather_x = TensorGather(attn_in, *scratch[10:12])
    gather_o = TensorGather(out_low, *scratch[12:14])

    def zcopy(w, way, step, blk, src):
        return remote(
            src, weights[w][1].at[blk * 2 + b], zsend.at[w, way, step],
            wrecv.at[w, blk * 2 + b], (line + (1 if way == 0 else -1)) * 2 + b, t,
        )

    def xcopy(w, blk, src):
        return remote(
            src, weights[w][1].at[blk * 2 + b], xsend.at[w, blk], wrecv.at[w, blk * 2 + b],
            line * 2 + (1 - b), t,
        )

    def local(w):
        return pltpu.make_async_copy(weights[w][0], weights[w][1].at[d], lsem.at[w])

    for w in range(4):
        own = weights[w][0]

        @pl.when(line + 1 < line_count)
        def _():
            zcopy(w, 0, 0, line, own).start()

        @pl.when(line > 0)
        def _():
            zcopy(w, 1, 0, line, own).start()

        xcopy(w, line, own).start()
        local(w).start()
    gather_o.start(og_ref[...])
    vsum.middle()
    vec = vsum.finish()
    vec_out[...] = vec
    normed = layer_normalize(x_ref[...], vec[0:1], vec[1:2])[0]
    gather_x.start(normed.astype(BF16))

    def relay(step, carry):
        for w in range(4):
            for way in range(2):
                blk = line - step if way == 0 else line + step
                valid = (blk >= 0) if way == 0 else (blk < line_count)
                more = (line + 1 < line_count) if way == 0 else (line > 0)

                @pl.when(valid)
                def _():
                    src = weights[w][1].at[blk * 2 + b]
                    zcopy(w, way, step, blk, src).wait_recv()

                    @pl.when(more)
                    def _():
                        zcopy(w, way, step, blk, src).start()

                    xcopy(w, blk, src).start()
        return carry

    lax.fori_loop(1, line_count, relay, 0)
    gather_o.forward()
    gather_x.forward()
    for w in range(4):
        local(w).wait()

        @pl.when(line + 1 < line_count)
        def _():
            zcopy(w, 0, 0, line, weights[w][0]).wait_send()

        @pl.when(line > 0)
        def _():
            zcopy(w, 1, 0, line, weights[w][0]).wait_send()

    def drain(step, carry):
        for w in range(4):
            for way in range(2):
                blk = line - step if way == 0 else line + step
                valid = (blk >= 0) if way == 0 else (blk < line_count)
                more = (line + 1 < line_count) if way == 0 else (line > 0)

                @pl.when(valid & more)
                def _():
                    zcopy(w, way, step, blk, weights[w][1].at[blk * 2 + b]).wait_send()
        return carry

    lax.fori_loop(1, line_count, drain, 0)

    def drain_x(blk, carry):
        for w in range(4):
            xcopy(w, blk, weights[w][0]).wait_send()
            remote(
                weights[w][0], weights[w][1].at[blk * 2 + (1 - b)], xsend.at[w, blk],
                wrecv.at[w, blk * 2 + (1 - b)], line * 2 + (1 - b), t,
            ).wait_recv()
        return carry

    lax.fori_loop(0, line_count, drain_x, 0)
    gather_o.finish()
    gather_x.finish()


def params(collective_id):
    return pltpu.CompilerParams(
        collective_id=collective_id, has_side_effects=True, vmem_limit_bytes=60 * 1024 * 1024
    )


def vmem(count):
    return [pl.BlockSpec(memory_space=pltpu.VMEM)] * count


def gather_all(dp_count, vec, x, og, weights):
    rows, width = x.shape
    line_count = dp_count // 2
    shape = jax.ShapeDtypeStruct
    return pl.pallas_call(
        functools.partial(gather_kernel, dp_count),
        out_shape=[
            shape(vec.shape, F32),
            shape((4, rows, width), BF16),
            shape((4, rows, width), BF16),
        ] + [shape((dp_count,) + w.shape, BF16) for w in weights],
        in_specs=vmem(7),
        out_specs=vmem(3) + [pl.BlockSpec(memory_space=pl.ANY)] * 4,
        scratch_shapes=[
            pltpu.SemaphoreType.DMA((4, 2, line_count)),
            pltpu.SemaphoreType.DMA((4, line_count)),
            pltpu.SemaphoreType.DMA((4, dp_count)),
            pltpu.SemaphoreType.DMA((4,)),
        ] + VectorSum.scratch(dp_count, width) + TensorGather.scratch() + TensorGather.scratch(),
        compiler_params=params(1),
        name="gather_all",
    )(vec, x, og, *weights)


def middle_kernel(part, x_ref, vec_ref, middle_ref, mlp_in, *scratch):
    enter(1)
    scatter = TensorScatter(part, *scratch[:5])
    gather = TensorGather(mlp_in, *scratch[5:7])
    scatter.start()
    scatter.middle()
    base = x_ref[...] + vec_ref[2:3]
    middle = base + scatter.finish()
    middle_ref[...] = middle
    gather.start(layer_normalize(middle, vec_ref[3:4], vec_ref[4:5])[0].astype(BF16))
    gather.forward()
    gather.finish()


def middle_exchange(part, x, vec):
    rows, width = x.shape
    shape = jax.ShapeDtypeStruct
    return pl.pallas_call(
        middle_kernel,
        out_shape=[shape(x.shape, F32), shape((4, rows, width), BF16)],
        in_specs=vmem(3),
        out_specs=vmem(2),
        scratch_shapes=TensorScatter.scratch(rows, width) + TensorGather.scratch(),
        compiler_params=params(2),
        name="middle_exchange",
    )(part, x, vec)


def put_rows(base, values):
    row = lax.broadcasted_iota(jnp.int32, base.shape, 0)
    for index, value in values:
        base = jnp.where(row == index, value, base)
    return base


def column_sum(value):
    return jnp.sum(value, axis=0, keepdims=True)


def back_kernel(part, middle_ref, run_ref, vec_ref, grad_ref, low, sums_ref, *scratch):
    enter(1)
    scatter = TensorScatter(part, *scratch[:5])
    gather = TensorGather(low, *scratch[5:7])
    scatter.start()
    scatter.middle()
    _, normed, inverse = layer_normalize(middle_ref[...], vec_ref[3:4], vec_ref[4:5])
    upstream = scatter.finish()
    grad = run_ref[...] + norm_backward_step(upstream, vec_ref[3:4], normed, inverse)
    grad_ref[...] = grad
    gather.start(grad.astype(BF16))
    sums_ref[...] = put_rows(
        jnp.zeros(sums_ref.shape, F32),
        [
            (2, column_sum(grad)),
            (3, column_sum(upstream * normed)),
            (4, column_sum(upstream)),
            (5, column_sum(run_ref[...])),
        ],
    )
    gather.forward()
    gather.finish()


def back_exchange(part, middle, run, vec):
    rows, width = middle.shape
    shape = jax.ShapeDtypeStruct
    return pl.pallas_call(
        back_kernel,
        out_shape=[
            shape(middle.shape, F32),
            shape((4, rows, width), BF16),
            shape((VECTOR_ROWS, width), F32),
        ],
        in_specs=vmem(4),
        out_specs=vmem(3),
        scratch_shapes=TensorScatter.scratch(rows, width) + TensorGather.scratch(),
        compiler_params=params(3),
        name="back_exchange",
    )(part, middle, run, vec)


def reduce_kernel(dp_count, *refs):
    (part_in, part_out, x_ref, middle_ref, mgrad_ref, vec_ref, sums_ref,
     g0, g1, g2, g3,
     block_out, input_grad, sums_out, o0, o1, o2, o3,
     *scratch) = refs
    grads, outs = (g0, g1, g2, g3), (o0, o1, o2, o3)
    held, below, above = scratch[0:4], scratch[4:8], scratch[8:12]
    xsend, xrecv, zsend, zrecv = scratch[12:16]
    vsum = VectorSum(dp_count, *scratch[16:22])
    d, t = place()
    line, b = d // 2, d % 2
    line_count = dp_count // 2
    enter(dp_count)
    scatter_in = TensorScatter(part_in, *scratch[22:27])
    scatter_out = TensorScatter(part_out, *scratch[27:32])

    def xcopy(w, target):
        return remote(
            grads[w].at[target * 2 + (1 - b)], held[w].at[target], xsend.at[w, target],
            xrecv.at[w, target], line * 2 + (1 - b), t,
        )

    def zcopy(w, way, target):
        dst = (below if way == 0 else above)[w]
        return remote(
            held[w].at[target], dst.at[target], zsend.at[w, target],
            zrecv.at[w, way, target], (line + (1 if way == 0 else -1)) * 2 + b, t,
        )

    def each_target(act):
        def step(i, carry):
            @pl.when(line_count - 1 - i > line)
            def _():
                act(0, line_count - 1 - i)

            @pl.when(i < line)
            def _():
                act(1, i)

            return carry

        lax.fori_loop(0, line_count - 1, step, 0)

    def send_x(way, target):
        for w in range(4):
            xcopy(w, target).start()

    scatter_in.start()
    each_target(send_x)
    send_x(0, line)
    scatter_in.middle()
    scatter_out.start()
    scatter_out.middle()
    _, normed, inverse = layer_normalize(x_ref[...], vec_ref[0:1], vec_ref[1:2])
    upstream = scatter_in.finish()
    input_grad[...] = mgrad_ref[...] + norm_backward_step(
        upstream, vec_ref[0:1], normed, inverse
    )
    vsum.start(
        put_rows(
            sums_ref[...], [(0, column_sum(upstream * normed)), (1, column_sum(upstream))]
        )
    )

    def reduce(way, target):
        for w in range(4):
            xcopy(w, target).wait_recv()
            dst = (below if way == 0 else above)[w]
            has = (line > 0) if way == 0 else (line + 1 < line_count)

            @pl.when(has)
            def _():
                zcopy(w, way, target).wait_recv()
                held[w][target] = (
                    grads[w][target * 2 + b].astype(F32)
                    + held[w][target].astype(F32)
                    + dst[target].astype(F32)
                ).astype(BF16)

            @pl.when(jnp.logical_not(has))
            def _():
                held[w][target] = (
                    grads[w][target * 2 + b].astype(F32) + held[w][target].astype(F32)
                ).astype(BF16)

            zcopy(w, way, target).start()

    each_target(reduce)
    block_out[...] = middle_ref[...] + scatter_out.finish() + vec_ref[5:6]
    vsum.middle()
    for w in range(4):
        xcopy(w, line).wait_recv()
        outs[w][...] = grads[w][d].astype(F32) + held[w][line].astype(F32)

        @pl.when(line > 0)
        def _():
            zcopy(w, 0, line).wait_recv()
            outs[w][...] += below[w][line].astype(F32)

        @pl.when(line + 1 < line_count)
        def _():
            zcopy(w, 1, line).wait_recv()
            outs[w][...] += above[w][line].astype(F32)

    sums_out[...] = vsum.finish()

    def drain(way, target):
        for w in range(4):
            zcopy(w, way, target).wait_send()
            xcopy(w, target).wait_send()

    each_target(drain)
    for w in range(4):
        xcopy(w, line).wait_send()


def reduce_all(dp_count, part_in, part_out, x, middle, mgrad, vec, sums, grads):
    rows, width = x.shape
    line_count = dp_count // 2
    shape = jax.ShapeDtypeStruct
    blocks = [g.shape[1:] for g in grads]
    lines = [pltpu.VMEM((line_count,) + s, BF16) for s in blocks]
    return pl.pallas_call(
        functools.partial(reduce_kernel, dp_count),
        out_shape=[shape(x.shape, F32), shape(x.shape, F32), shape(vec.shape, F32)]
        + [shape(s, F32) for s in blocks],
        in_specs=vmem(11),
        out_specs=vmem(7),
        scratch_shapes=lines * 3
        + [
            pltpu.SemaphoreType.DMA((4, line_count)),
            pltpu.SemaphoreType.DMA((4, line_count)),
            pltpu.SemaphoreType.DMA((4, line_count)),
            pltpu.SemaphoreType.DMA((4, 2, line_count)),
        ]
        + VectorSum.scratch(dp_count, width)
        + TensorScatter.scratch(rows, width)
        + TensorScatter.scratch(rows, width),
        compiler_params=params(4),
        name="reduce_all",
    )(part_in, part_out, x, middle, mgrad, vec, sums, *grads)


def per_device(
    dp_count,
    block_input,
    seq_begin,
    group_fill,
    attention_norm_gain,
    attention_norm_bias,
    qkv_weight,
    qv_bias,
    dense_weight,
    dense_bias,
    feedforward_norm_gain,
    feedforward_norm_bias,
    up_weight,
    up_bias,
    down_weight,
    down_bias,
    out_grad,
):
    head_dim = D // HEADS
    own_rows, width = block_input.shape
    group_rows = seq_begin.shape[0]
    dp_index, tensor_index = lax.axis_index("dp"), lax.axis_index("tensor")
    shard = dp_index * 4 + tensor_index
    norm_vectors = jnp.stack(
        [
            attention_norm_gain,
            attention_norm_bias,
            dense_bias,
            feedforward_norm_gain,
            feedforward_norm_bias,
            down_bias,
        ]
    )
    piece = norm_vectors.shape[1]
    up_piece, qv_piece = up_bias.shape[0], qv_bias.shape[0]
    vec = jnp.zeros((VECTOR_ROWS, width), F32)
    vec = lax.dynamic_update_slice(vec, norm_vectors, (0, shard * piece))
    vec = lax.dynamic_update_slice(vec, up_bias.astype(F32)[None], (6, dp_index * up_piece))
    vec = lax.dynamic_update_slice(vec, qv_bias.astype(F32)[None], (7, dp_index * qv_piece))
    row_ids = tensor_index * own_rows + jnp.arange(own_rows, dtype=jnp.int32)
    live_rows = (row_ids < group_fill[0]).astype(jnp.float32)[:, None]
    running_gradient = out_grad * live_rows
    vec, attn_in, out_low, qkv_full, dense_full, up_full, down_full = gather_all(
        dp_count,
        vec,
        block_input,
        running_gradient.astype(BF16),
        (qkv_weight, dense_weight, up_weight, down_weight),
    )
    attn_in = attn_in.reshape(group_rows, width)
    out_low = out_low.reshape(group_rows, width)
    qkv_full, dense_full, up_full, down_full = (
        w.reshape(-1, w.shape[-1]) for w in (qkv_full, dense_full, up_full, down_full)
    )
    local_heads = qkv_full.shape[1] // (3 * head_dim)
    slopes = head_slopes((tensor_index * local_heads).astype(jnp.float32), local_heads)
    projected = jnp.dot(attn_in, qkv_full, preferred_element_type=jnp.float32).reshape(
        group_rows, local_heads, 3, head_dim
    )
    bias_pair = vec[7, : 2 * local_heads * head_dim].reshape(local_heads, 2, head_dim)
    bias_full = jnp.stack(
        [bias_pair[:, 0], jnp.zeros_like(bias_pair[:, 0]), bias_pair[:, 1]], axis=1
    )
    qkv_low = (projected + bias_full).astype(jnp.bfloat16)
    queries = qkv_low[:, :, 0]
    key_all = qkv_low[:, :, 1]
    values = qkv_low[:, :, 2]
    context, log_total = attention_forward(queries, key_all, values, slopes, seq_begin)
    context_flat = context.reshape(group_rows, local_heads * head_dim)
    attn_part = jnp.dot(context_flat, dense_full, preferred_element_type=jnp.float32).astype(BF16)
    residual_middle, mlp_in = middle_exchange(
        attn_part.reshape(4, own_rows, width), block_input, vec
    )
    mlp_in = mlp_in.reshape(group_rows, width)
    pre_act = jnp.dot(mlp_in, up_full, preferred_element_type=jnp.float32) + vec[6]
    act_value, act_back = jax.vjp(gelu_tanh, pre_act)
    activated = act_value.astype(jnp.bfloat16)
    act_grad = lax.dot_general(
        out_low, down_full, CONTRACT_COLS, preferred_element_type=jnp.float32
    )
    pre_grad = act_back(act_grad)[0].astype(jnp.bfloat16)
    mlp_in_part = lax.dot_general(
        pre_grad, up_full, CONTRACT_COLS, preferred_element_type=jnp.float32
    ).astype(BF16)
    residual_middle_gradient, middle_low, sums = back_exchange(
        mlp_in_part.reshape(4, own_rows, width), residual_middle, running_gradient, vec
    )
    middle_low = middle_low.reshape(group_rows, width)
    mlp_part = jnp.dot(activated, down_full, preferred_element_type=jnp.float32).astype(BF16)
    down_grad = lax.dot_general(
        activated, out_low, CONTRACT_ROWS, preferred_element_type=jnp.float32
    )
    up_grad = lax.dot_general(mlp_in, pre_grad, CONTRACT_ROWS, preferred_element_type=jnp.float32)
    up_shift_grad = jnp.sum(pre_grad.astype(jnp.float32), axis=0)
    dense_grad = lax.dot_general(
        context_flat, middle_low, CONTRACT_ROWS, preferred_element_type=jnp.float32
    )
    context_grad = lax.dot_general(
        middle_low, dense_full, CONTRACT_COLS, preferred_element_type=jnp.float32
    )
    context_grad = context_grad.astype(jnp.bfloat16).reshape(group_rows, local_heads, head_dim)
    qkv_grad = attention_backward(
        queries, key_all, values, slopes, seq_begin, log_total, context, context_grad
    )
    qkv_grad_flat = qkv_grad.reshape(group_rows, 3 * local_heads * head_dim)
    qkv_grad_sum = lax.dot_general(
        attn_in, qkv_grad_flat, CONTRACT_ROWS, preferred_element_type=jnp.float32
    )
    summed = jnp.sum(qkv_grad.astype(jnp.float32), axis=0)
    qv_grad = jnp.stack([summed[:, 0], summed[:, 2]], axis=1).reshape(2 * local_heads * head_dim)
    attn_in_part = lax.dot_general(
        qkv_grad_flat, qkv_full, CONTRACT_COLS, preferred_element_type=jnp.float32
    ).astype(BF16)
    sums = lax.dynamic_update_slice(sums, up_shift_grad[None], (6, 0))
    sums = lax.dynamic_update_slice(sums, qv_grad[None], (7, 0))
    grads = tuple(
        g.astype(BF16).reshape(dp_count, -1, g.shape[-1])
        for g in (qkv_grad_sum, dense_grad, up_grad, down_grad)
    )
    block_out, block_input_gradient, sums, qkv_out, dense_out, up_out, down_out = reduce_all(
        dp_count,
        attn_in_part.reshape(4, own_rows, width),
        mlp_part.reshape(4, own_rows, width),
        block_input,
        residual_middle,
        residual_middle_gradient,
        vec,
        sums,
        grads,
    )
    vectors = lax.dynamic_slice(sums, (0, shard * piece), (6, piece))
    up_shift_out = lax.dynamic_slice(sums, (6, dp_index * up_piece), (1, up_piece))[0]
    qv_out = lax.dynamic_slice(sums, (7, dp_index * qv_piece), (1, qv_piece))[0]
    return (
        block_out,
        block_input_gradient,
        vectors[0],
        vectors[1],
        qkv_out,
        qv_out,
        dense_out,
        vectors[2],
        vectors[3],
        vectors[4],
        up_out,
        up_shift_out,
        down_out,
        vectors[5],
    )


def solution(mesh):
    return jax.shard_map(
        functools.partial(per_device, mesh.shape["dp"]),
        mesh=mesh,
        in_specs=(
            P(("dp", "tensor"), None),
            P("dp"),
            P("dp"),
            P(("dp", "tensor")),
            P(("dp", "tensor")),
            P("dp", "tensor"),
            P(("tensor", "dp")),
            P(("tensor", "dp"), None),
            P(("dp", "tensor")),
            P(("dp", "tensor")),
            P(("dp", "tensor")),
            P("dp", "tensor"),
            P(("tensor", "dp")),
            P(("tensor", "dp"), None),
            P(("dp", "tensor")),
            P(("dp", "tensor"), None),
        ),
        out_specs=(
            P(("dp", "tensor"), None),
            P(("dp", "tensor"), None),
            P(("dp", "tensor")),
            P(("dp", "tensor")),
            P("dp", "tensor"),
            P(("tensor", "dp")),
            P(("tensor", "dp"), None),
            P(("dp", "tensor")),
            P(("dp", "tensor")),
            P(("dp", "tensor")),
            P("dp", "tensor"),
            P(("tensor", "dp")),
            P(("tensor", "dp"), None),
            P(("dp", "tensor")),
        ),
        check_vma=False,
    )
```

time: 747 us -> 272 us (0.36)
  waiting for transfers between devices: 472 us -> 0 us
  Pallas kernels: 0 us -> 208 us
  blocking collectives: 176 us -> 0 us
  between operations: 16.9 us -> 1.63 us
  matrix products: 47.9 us -> 34.7 us
  other arithmetic: 16 us -> 5.89 us
    reduce_scatter x8 -> x0, waiting for transfers between devices: 336 us -> none  [the longest x1 92 us: per_device(): lax.psum_scatter(down_grad, 'dp', scatter_dimension=0, tiled=True)]
    pallas_call x0 -> x4, Pallas kernels: none -> 208 us  [the longest x1 83.7 us: reduce_all(): pl.pallas_call(functools.partial(reduce_kernel, dp_count), out_shape=[sha...]
    all_gather x7 -> x0, waiting for transfers between devices: 134 us -> none  [the longest x1 51.2 us: per_device(): lax.all_gather(down_weight, 'dp', axis=0, tiled=True)]
    unnamed x4 -> x0, blocking collectives: 123 us -> none
    all_gather x2 -> x0, blocking collectives: 53.4 us -> none  [the longest x1 32.6 us: per_device(): lax.all_gather(dense_weight, 'dp', axis=0, tiled=True)]
    unnamed x57 -> x38, local copies, waits for them, and re-layouts: 15.9 us -> 8.79 us
  transfers between devices with their start and end apart: 15 -> 0, of which waited for: 12 -> 0; matrix products, arithmetic and copies ran while one was open for 5% -> 0% of each run, Pallas kernels for 0% -> 0%
where the time goes in v1:
time: 272 us; the launch traced here: 271 us
  Pallas kernels  208 us (76%)
  matrix products  34.7 us (13%)
  local copies, waits for them, and re-layouts  20.9 us (8%)
  other arithmetic  5.89 us (2%)
    pallas_call x1, Pallas kernels, reduce_all(): pl.pallas_call(functools.partial(reduce_kernel, dp_count), out_shape=[sha...  83.7 us
    pallas_call x1, Pallas kernels, gather_all(): pl.pallas_call(functools.partial(gather_kernel, dp_count), out_shape=[sha...  81.4 us
    pallas_call x1, Pallas kernels, middle_exchange(): pl.pallas_call(middle_kernel, out_shape=[shape(x.shape, F32), shape((4, r...  21.7 us
    pallas_call x1, Pallas kernels, back_exchange(): pl.pallas_call(back_kernel, out_shape=[shape(middle.shape, F32), shape((4...  21.2 us
    unnamed x38, local copies, waits for them, and re-layouts  8.79 us

profile of v1, /device:TPU:0, one launch (start us, length us, event | category | flops | bytes accessed | tf_op | source)
XLA Modules:
  0.0 271.3 jit_solution(2410562895470316759)
XLA Ops:
  1.3 0.7 bitcast_convert_fusion
  2.0 0.7 bitcast_convert_fusion.1
  2.6 0.1 pad.6.clone
  2.7 0.8 stack.49
  3.5 0.4 dynamic_update_slice.15
  3.9 0.2 dynamic_update_slice.16
  4.2 0.2 dynamic_update_slice.17.refs_0_
  4.4 0.0 copy-start.9
  4.4 1.5 fusion.13
  6.0 2.0 fusion.17
  8.0 0.1 subtract_convert_fusion
  8.1 0.0 copy-done.9
  8.1 81.4 %gather_all.1 = (f32[8,1024]{1,0:T(8,128)}, bf16[4,128,1024]{2,1,0:T(8,128)(2,1)}, bf16[4,128,1024]{2,1,0:T(8,128)(2,1)}, bf16[8,128,768]{2,1,0:T(8,128)(2,1)}, ...) custom-call(f32[8,1024]{1,0:T(8,128)} %copy-done.9, ...), custom_call_target="tpu_custom_call" | custom-call | tf_op jit(solution)/shard_map/gather_all/pallas_call | solution.py:428
  89.5 0.7 slice_reduce_fusion
  90.3 0.1 reshape_squeeze.3
  90.4 0.1 pad_maximum_fusion.1
  90.4 0.8 slice.51
  91.2 1.9 copy.43
  93.1 0.0 copy-start.8
  93.1 2.3 add_convert_fusion
  95.4 0.0 copy-done.8
  95.4 1.3 fusion.20
  96.7 0.0 copy-start
  96.7 0.6 exponential_reduce_fusion
  97.3 1.3 copy-done
  98.7 0.8 convolution_convert_fusion.10
  99.5 0.3 copy-done.4
  99.7 1.4 convolution_convert_fusion.6
  101.2 21.7 %middle_exchange.1 = (f32[128,1024]{1,0:T(8,128)}, bf16[4,128,1024]{2,1,0:T(8,128)(2,1)}) custom-call(bf16[4,128,1024]{2,1,0:T(8,128)(2,1)} %bitcast.118, f32[128,1024]{1,0:T(8,128)} %refs_2_.1, f32[8,1024]{1,0:T(8,128)} %get-tuple-element.35.vec_ref.refs_5_), custom_call_target="tpu_custom_call" | custom-call | tf_op jit(solution)/shard_map/middle_exchange/pallas_call | solution.py:465
  122.9 0.0 copy-start.12
  122.9 3.3 %fusion.21 = f32[512,1024]{1,0:T(8,128)S(1)} fusion(bf16[512,1024]{1,0:T(8,128)(2,1)} %bitcast.156, bf16[1024,1024]{1,0:T(8,128)(2,1)} %bitcast.150), kind=kOutput, calls=%fused_computation.67 | convolution fusion | flops 1073741824 | bytes 5242880 | tf_op jit(solution)/shard_map/dot_general | solution.py:747
  126.2 2.5 convolution_convert_fusion.4
  128.8 2.5 convert_reduce_fusion
  131.3 3.0 %convolution_convert_fusion = bf16[1024,1024]{1,0:T(8,128)(2,1)} fusion(bf16[512,1024]{1,0:T(8,128)(2,1)S(1)} %bitcast.159, f32[512,1024]{1,0:T(8,128)S(1)} %fusion.21, f32[1024]{0:T(1024)S(1)} %bitcast.142), kind=kOutput, calls=%fused_computation.16 | convolution fusion | flops 1080033280 | bytes 5246976 | tf_op jit(solution)/shard_map/dot_general | solution.py:762
  134.3 2.3 convolution_convert_fusion.5
  136.6 21.2 %back_exchange.1 = (f32[128,1024]{1,0:T(8,128)}, bf16[4,128,1024]{2,1,0:T(8,128)(2,1)}, f32[8,1024]{1,0:T(8,128)}) custom-call(bf16[4,128,1024]{2,1,0:T(8,128)(2,1)} %bitcast.132, f32[128,1024]{1,0:T(8,128)} %get-tuple-element.41.middle_ref.refs_3_, f32[128,1024]{1,0:T(8,128)} %get-tuple-element.57.run_ref, f32[8,1024]{1,0:T(8,128)} %get-tuple-element.35.vec_ref.refs_5_), custom_call_target="tpu_custom_call" | custom-call | tf_op jit(solution)/shard_map/back_exchange/pallas_call | solution.py:514
  157.8 1.8 multiply_reduce_fusion
  159.6 1.2 convolution_convert_fusion.7
  160.9 1.4 dynamic_update_slice.18
  162.3 3.1 %fusion.12 = bf16[512,4,1,64]{0,3,1,2:T(8,128)(2,1)S(1)} fusion(bf16[512,4,64]{0,2,1:T(8,128)(2,1)S(1)} %bitcast.133, f32[4,512,512]{1,2,0:T(8,128)} %copy-done, f32[4,512]{1,0:T(4,128)S(1)} %log_add_fusion), kind=kOutput, calls=%fused_computation.35 | convolution fusion | flops 136445952 | bytes 4726784 | tf_op jit(solution)/shard_map/hqk,qhd->khd/dot_general | solution.py:81
  165.4 0.3 copy-done.1
  165.7 1.1 multiply_convert_fusion
  166.8 0.8 fusion.10
  167.5 0.5 fusion.11
  168.0 0.2 convert_reduce_fusion.1
  168.2 0.1 broadcast_in_dim_reshape.3
  168.3 1.5 dynamic_update_slice.19.refs_6_
  169.8 0.1 copy.49
  169.9 2.0 convolution_convert_fusion.3
  171.9 0.0 copy-done.13
  171.9 2.2 convolution_convert_fusion.2
  174.1 2.6 convolution_convert_fusion.1
  176.8 83.7 %reduce_all.1 = (f32[128,1024]{1,0:T(8,128)}, f32[128,1024]{1,0:T(8,128)}, f32[8,1024]{1,0:T(8,128)}, f32[128,768]{1,0:T(8,128)}, f32[32,1024]{1,0:T(8,128)}, /*index=5*/f32[128,1024]{1,0:T(8,128)}, f32[128,1024]{1,0:T(8,128)}) custom-call(bf16[4,128,1024]{2,1,0:T(8,128)(2,1)} %bitcast.129, bf16[4,128,1024]{2,1,0:T(8,128)(2,1)} %bitcast.128, ...), custom_call_target="tpu_custom_call" | custom-call | tf_op jit(solution)/shard_map/reduce_all/pallas_call | solution.py:651
  260.6 1.3 dynamic-slice_bitcast_fusion
  261.9 1.2 dynamic-slice_bitcast_fusion.1
  263.1 0.7 constant_dynamic-slice_fusion
  263.9 0.5 slice_bitcast_fusion.9
  264.4 1.9 copy.69
  266.4 1.9 copy.70
  268.3 0.0 copy-done.7
  268.3 0.7 copy.71
  269.0 0.7 copy.72
  269.7 0.8 copy.73
  270.5 0.8 copy.74
  (29 shorter events, 0.1 us)
Async XLA Ops:
  4.4 3.7 %copy-start.9 = (f32[8,1024]{1,0:T(8,128)}, f32[8,1024]{1,0:T(8,128)S(1)}, u32[]{:S(2)}) copy-start(f32[8,1024]{1,0:T(8,128)S(1)} %dynamic_update_slice.17.refs_0_) | copy-start | bytes 98308
  93.1 2.3 copy-start.8
  96.7 1.9 copy-start
  98.7 1.0 copy-start.4
  122.9 3.3 %copy-start.12 = (bf16[8,128,1024]{2,1,0:T(8,128)(2,1)S(1)}, bf16[8,128,1024]{2,1,0:T(8,128)(2,1)}, u32[]{:S(2)}) copy-start(bf16[8,128,1024]{2,1,0:T(8,128)(2,1)} %get-tuple-element.37) | copy-start | bytes 6291460
  126.2 2.5 copy-start.15
  131.3 3.0 %copy-start.11 = (bf16[8,128,1024]{2,1,0:T(8,128)(2,1)S(1)}, bf16[8,128,1024]{2,1,0:T(8,128)(2,1)}, u32[]{:S(2)}) copy-start(bf16[8,128,1024]{2,1,0:T(8,128)(2,1)} %get-tuple-element.40) | copy-start | bytes 6291460
  157.8 1.8 copy-start.3
  162.2 3.4 %copy-start.1 = (f32[4,512,512]{1,2,0:T(8,128)S(1)}, f32[4,512,512]{1,2,0:T(8,128)}, u32[]{:S(2)}) copy-start(f32[4,512,512]{1,2,0:T(8,128)} %copy-done) | copy-start | bytes 12582916
  168.0 1.9 copy-start.2
  169.9 2.0 copy-start.13
  171.9 2.2 copy-start.14
  260.5 7.7 %copy-start.7 = (f32[128,768]{1,0:T(8,128)S(1)}, f32[128,768]{1,0:T(8,128)}, u32[]{:S(2)}) copy-start(f32[128,768]{1,0:T(8,128)} %get-tuple-element.90) | copy-start | bytes 1179652
  260.5 8.5 %copy-start.10 = (f32[32,1024]{1,0:T(8,128)S(1)}, f32[32,1024]{1,0:T(8,128)}, u32[]{:S(2)}) copy-start(f32[32,1024]{1,0:T(8,128)} %get-tuple-element.92) | copy-start | bytes 393220
  260.6 9.1 %copy-start.6 = (f32[128,1024]{1,0:T(8,128)S(1)}, f32[128,1024]{1,0:T(8,128)}, u32[]{:S(2)}) copy-start(f32[128,1024]{1,0:T(8,128)} %get-tuple-element.96) | copy-start | bytes 1572868
  264.4 6.0 %copy-start.5 = (f32[128,1024]{1,0:T(8,128)S(1)}, f32[128,1024]{1,0:T(8,128)}, u32[]{:S(2)}) copy-start(f32[128,1024]{1,0:T(8,128)} %get-tuple-element.98) | copy-start | bytes 1572868

commit v2 on v1

--- a/solution.py
+++ b/solution.py
@@ -300,113 +300,238 @@
         )
 
 
+class LineGather:
+    def __init__(self, dp_count, weights, zsend, xsend, wrecv, lsem):
+        self.weights, self.line_count = weights, dp_count // 2
+        self.zsend, self.xsend, self.wrecv, self.lsem = zsend, xsend, wrecv, lsem
+        self.d, self.t = place()
+        self.line, self.b = self.d // 2, self.d % 2
+
+    @staticmethod
+    def scratch(dp_count, count):
+        return [
+            pltpu.SemaphoreType.DMA((count, 2, dp_count // 2)),
+            pltpu.SemaphoreType.DMA((count, dp_count // 2)),
+            pltpu.SemaphoreType.DMA((count, dp_count)),
+            pltpu.SemaphoreType.DMA((count,)),
+        ]
+
+    def zcopy(self, w, way, step, blk, src):
+        slot = blk * 2 + self.b
+        return remote(
+            src, self.weights[w][1].at[slot], self.zsend.at[w, way, step],
+            self.wrecv.at[w, slot], (self.line + (1 if way == 0 else -1)) * 2 + self.b, self.t,
+        )
+
+    def xcopy(self, w, blk, b, src):
+        slot = blk * 2 + b
+        return remote(
+            src, self.weights[w][1].at[slot], self.xsend.at[w, blk], self.wrecv.at[w, slot],
+            self.line * 2 + (1 - self.b), self.t,
+        )
+
+    def local(self, w):
+        return pltpu.make_async_copy(self.weights[w][0], self.weights[w][1].at[self.d], self.lsem.at[w])
+
+    def more(self, way):
+        return (self.line + 1 < self.line_count) if way == 0 else (self.line > 0)
+
+    def start(self):
+        for w in range(len(self.weights)):
+            own = self.weights[w][0]
+            for way in range(2):
+
+                @pl.when(self.more(way))
+                def _():
+                    self.zcopy(w, way, 0, self.line, own).start()
+
+            self.xcopy(w, self.line, self.b, own).start()
+            self.local(w).start()
+
+    def hops(self, act, sending=False):
+        def hop(step, carry):
+            for w in range(len(self.weights)):
+                for way in range(2):
+                    blk = self.line - step if way == 0 else self.line + step
+
+                    valid = (blk >= 0) if way == 0 else (blk < self.line_count)
+                    if sending:
+                        valid = valid & self.more(way)
+
+                    @pl.when(valid)
+                    def _():
+                        act(w, way, step, blk, self.weights[w][1].at[blk * 2 + self.b])
+
+            return carry
+
+        lax.fori_loop(1, self.line_count, hop, 0)
+
+    def relay(self):
+        def act(w, way, step, blk, src):
+            self.zcopy(w, way, step, blk, src).wait_recv()
+
+            @pl.when(self.more(way))
+            def _():
+                self.zcopy(w, way, step, blk, src).start()
+
+            self.xcopy(w, blk, self.b, src).start()
+
+        self.hops(act)
+
+    def finish(self):
+        for w in range(len(self.weights)):
+            self.local(w).wait()
+            for way in range(2):
+
+                @pl.when(self.more(way))
+                def _():
+                    self.zcopy(w, way, 0, self.line, self.weights[w][0]).wait_send()
+
+        def act(w, way, step, blk, src):
+            self.zcopy(w, way, step, blk, src).wait_send()
+
+        self.hops(act, sending=True)
+
+        def pair(blk, carry):
+            for w in range(len(self.weights)):
+                own = self.weights[w][0]
+                self.xcopy(w, blk, self.b, own).wait_send()
+                self.xcopy(w, blk, 1 - self.b, own).wait_recv()
+            return carry
+
+        lax.fori_loop(0, self.line_count, pair, 0)
+
+
+class LineReduce:
+    def __init__(self, dp_count, grads, outs, buffers, xsend, xrecv, zsend, zrecv):
+        n = len(grads)
+        self.n, self.grads, self.outs = n, grads, outs
+        self.held, self.below, self.above = buffers[:n], buffers[n : 2 * n], buffers[2 * n :]
+        self.xsend, self.xrecv, self.zsend, self.zrecv = xsend, xrecv, zsend, zrecv
+        self.line_count = dp_count // 2
+        self.d, self.t = place()
+        self.line, self.b = self.d // 2, self.d % 2
+
+    @staticmethod
+    def scratch(dp_count, blocks):
+        line_count, n = dp_count // 2, len(blocks)
+        return [pltpu.VMEM((line_count,) + s, BF16) for s in blocks] * 3 + [
+            pltpu.SemaphoreType.DMA((n, line_count)),
+            pltpu.SemaphoreType.DMA((n, line_count)),
+            pltpu.SemaphoreType.DMA((n, line_count)),
+            pltpu.SemaphoreType.DMA((n, 2, line_count)),
+        ]
+
+    def xcopy(self, w, target):
+        return remote(
+            self.grads[w].at[target * 2 + (1 - self.b)], self.held[w].at[target],
+            self.xsend.at[w, target], self.xrecv.at[w, target],
+            self.line * 2 + (1 - self.b), self.t,
+        )
+
+    def zcopy(self, w, way, target):
+        dst = (self.below if way == 0 else self.above)[w]
+        return remote(
+            self.held[w].at[target], dst.at[target], self.zsend.at[w, target],
+            self.zrecv.at[w, way, target],
+            (self.line + (1 if way == 0 else -1)) * 2 + self.b, self.t,
+        )
+
+    def each_target(self, act):
+        last = self.line_count - 1
+
+        def step(i, carry):
+            @pl.when(last - i > self.line)
+            def _():
+                act(0, last - i)
+
+            @pl.when(i < self.line)
+            def _():
+                act(1, i)
+
+            return carry
+
+        lax.fori_loop(0, last, step, 0)
+
+    def start(self):
+        def send(way, target):
+            for w in range(self.n):
+                self.xcopy(w, target).start()
+
+        self.each_target(send)
+        send(0, self.line)
+
+    def has(self, way):
+        return (self.line > 0) if way == 0 else (self.line + 1 < self.line_count)
+
+    def run(self):
+        def reduce(way, target):
+            for w in range(self.n):
+                self.xcopy(w, target).wait_recv()
+                dst = (self.below if way == 0 else self.above)[w]
+                held, grad = self.held[w], self.grads[w]
+
+                @pl.when(self.has(way))
+                def _():
+                    self.zcopy(w, way, target).wait_recv()
+                    held[target] = (
+                        grad[target * 2 + self.b].astype(F32)
+                        + held[target].astype(F32)
+                        + dst[target].astype(F32)
+                    ).astype(BF16)
+
+                @pl.when(jnp.logical_not(self.has(way)))
+                def _():
+                    held[target] = (
+                        grad[target * 2 + self.b].astype(F32) + held[target].astype(F32)
+                    ).astype(BF16)
+
+                self.zcopy(w, way, target).start()
+
+        self.each_target(reduce)
+
+    def finish(self):
+        for w in range(self.n):
+            self.xcopy(w, self.line).wait_recv()
+            out = self.outs[w]
+            out[...] = self.grads[w][self.d].astype(F32) + self.held[w][self.line].astype(F32)
+            for way in range(2):
+
+                @pl.when(self.has(way))
+                def _():
+                    self.zcopy(w, way, self.line).wait_recv()
+                    out[...] += (self.below if way == 0 else self.above)[w][self.line].astype(F32)
+
+    def drain(self):
+        def act(way, target):
+            for w in range(self.n):
+                self.zcopy(w, way, target).wait_send()
+                self.xcopy(w, target).wait_send()
+
+        self.each_target(act)
+        for w in range(self.n):
+            self.xcopy(w, self.line).wait_send()
+
+
 def gather_kernel(dp_count, *refs):
-    (vec_ref, x_ref, og_ref, w0, w1, w2, w3,
-     vec_out, attn_in, out_low, o0, o1, o2, o3,
-     *scratch) = refs
-    weights = list(zip((w0, w1, w2, w3), (o0, o1, o2, o3)))
-    zsend, xsend, wrecv, lsem = scratch[:4]
+    vec_ref, x_ref, og_ref, w0, w1, vec_out, attn_in, out_low, o0, o1, *scratch = refs
+    enter(dp_count)
     vsum = VectorSum(dp_count, *scratch[4:10])
-    d, t = place()
-    line, b = d // 2, d % 2
-    line_count = dp_count // 2
-    enter(dp_count)
     vsum.start(vec_ref[...])
+    weights = LineGather(dp_count, [(w0, o0), (w1, o1)], *scratch[:4])
     gather_x = TensorGather(attn_in, *scratch[10:12])
     gather_o = TensorGather(out_low, *scratch[12:14])
-
-    def zcopy(w, way, step, blk, src):
-        return remote(
-            src, weights[w][1].at[blk * 2 + b], zsend.at[w, way, step],
-            wrecv.at[w, blk * 2 + b], (line + (1 if way == 0 else -1)) * 2 + b, t,
-        )
-
-    def xcopy(w, blk, src):
-        return remote(
-            src, weights[w][1].at[blk * 2 + b], xsend.at[w, blk], wrecv.at[w, blk * 2 + b],
-            line * 2 + (1 - b), t,
-        )
-
-    def local(w):
-        return pltpu.make_async_copy(weights[w][0], weights[w][1].at[d], lsem.at[w])
-
-    for w in range(4):
-        own = weights[w][0]
-
-        @pl.when(line + 1 < line_count)
-        def _():
-            zcopy(w, 0, 0, line, own).start()
-
-        @pl.when(line > 0)
-        def _():
-            zcopy(w, 1, 0, line, own).start()
-
-        xcopy(w, line, own).start()
-        local(w).start()
+    weights.start()
     gather_o.start(og_ref[...])
     vsum.middle()
     vec = vsum.finish()
     vec_out[...] = vec
     normed = layer_normalize(x_ref[...], vec[0:1], vec[1:2])[0]
     gather_x.start(normed.astype(BF16))
-
-    def relay(step, carry):
-        for w in range(4):
-            for way in range(2):
-                blk = line - step if way == 0 else line + step
-                valid = (blk >= 0) if way == 0 else (blk < line_count)
-                more = (line + 1 < line_count) if way == 0 else (line > 0)
-
-                @pl.when(valid)
-                def _():
-                    src = weights[w][1].at[blk * 2 + b]
-                    zcopy(w, way, step, blk, src).wait_recv()
-
-                    @pl.when(more)
-                    def _():
-                        zcopy(w, way, step, blk, src).start()
-
-                    xcopy(w, blk, src).start()
-        return carry
-
-    lax.fori_loop(1, line_count, relay, 0)
+    weights.relay()
     gather_o.forward()
     gather_x.forward()
-    for w in range(4):
-        local(w).wait()
-
-        @pl.when(line + 1 < line_count)
-        def _():
-            zcopy(w, 0, 0, line, weights[w][0]).wait_send()
-
-        @pl.when(line > 0)
-        def _():
-            zcopy(w, 1, 0, line, weights[w][0]).wait_send()
-
-    def drain(step, carry):
-        for w in range(4):
-            for way in range(2):
-                blk = line - step if way == 0 else line + step
-                valid = (blk >= 0) if way == 0 else (blk < line_count)
-                more = (line + 1 < line_count) if way == 0 else (line > 0)
-
-                @pl.when(valid & more)
-                def _():
-                    zcopy(w, way, step, blk, weights[w][1].at[blk * 2 + b]).wait_send()
-        return carry
-
-    lax.fori_loop(1, line_count, drain, 0)
-
-    def drain_x(blk, carry):
-        for w in range(4):
-            xcopy(w, blk, weights[w][0]).wait_send()
-            remote(
-                weights[w][0], weights[w][1].at[blk * 2 + (1 - b)], xsend.at[w, blk],
-                wrecv.at[w, blk * 2 + (1 - b)], line * 2 + (1 - b), t,
-            ).wait_recv()
-        return carry
-
-    lax.fori_loop(0, line_count, drain_x, 0)
+    weights.finish()
     gather_o.finish()
     gather_x.finish()
 
@@ -421,9 +546,12 @@
     return [pl.BlockSpec(memory_space=pltpu.VMEM)] * count
 
 
+def hbm(count):
+    return [pl.BlockSpec(memory_space=pl.ANY)] * count
+
+
 def gather_all(dp_count, vec, x, og, weights):
     rows, width = x.shape
-    line_count = dp_count // 2
     shape = jax.ShapeDtypeStruct
     return pl.pallas_call(
         functools.partial(gather_kernel, dp_count),
@@ -432,45 +560,51 @@
             shape((4, rows, width), BF16),
             shape((4, rows, width), BF16),
         ] + [shape((dp_count,) + w.shape, BF16) for w in weights],
-        in_specs=vmem(7),
-        out_specs=vmem(3) + [pl.BlockSpec(memory_space=pl.ANY)] * 4,
-        scratch_shapes=[
-            pltpu.SemaphoreType.DMA((4, 2, line_count)),
-            pltpu.SemaphoreType.DMA((4, line_count)),
-            pltpu.SemaphoreType.DMA((4, dp_count)),
-            pltpu.SemaphoreType.DMA((4,)),
-        ] + VectorSum.scratch(dp_count, width) + TensorGather.scratch() + TensorGather.scratch(),
+        in_specs=vmem(5),
+        out_specs=vmem(3) + hbm(2),
+        scratch_shapes=LineGather.scratch(dp_count, 2)
+        + VectorSum.scratch(dp_count, width)
+        + TensorGather.scratch()
+        + TensorGather.scratch(),
         compiler_params=params(1),
         name="gather_all",
     )(vec, x, og, *weights)
 
 
-def middle_kernel(part, x_ref, vec_ref, middle_ref, mlp_in, *scratch):
-    enter(1)
+def middle_kernel(dp_count, *refs):
+    part, x_ref, vec_ref, w0, w1, middle_ref, mlp_in, o0, o1, *scratch = refs
+    enter(dp_count)
     scatter = TensorScatter(part, *scratch[:5])
     gather = TensorGather(mlp_in, *scratch[5:7])
+    weights = LineGather(dp_count, [(w0, o0), (w1, o1)], *scratch[7:11])
     scatter.start()
+    weights.start()
     scatter.middle()
     base = x_ref[...] + vec_ref[2:3]
     middle = base + scatter.finish()
     middle_ref[...] = middle
     gather.start(layer_normalize(middle, vec_ref[3:4], vec_ref[4:5])[0].astype(BF16))
+    weights.relay()
     gather.forward()
+    weights.finish()
     gather.finish()
 
 
-def middle_exchange(part, x, vec):
+def middle_exchange(dp_count, part, x, vec, weights):
     rows, width = x.shape
     shape = jax.ShapeDtypeStruct
     return pl.pallas_call(
-        middle_kernel,
-        out_shape=[shape(x.shape, F32), shape((4, rows, width), BF16)],
-        in_specs=vmem(3),
-        out_specs=vmem(2),
-        scratch_shapes=TensorScatter.scratch(rows, width) + TensorGather.scratch(),
+        functools.partial(middle_kernel, dp_count),
+        out_shape=[shape(x.shape, F32), shape((4, rows, width), BF16)]
+        + [shape((dp_count,) + w.shape, BF16) for w in weights],
+        in_specs=vmem(5),
+        out_specs=vmem(2) + hbm(2),
+        scratch_shapes=TensorScatter.scratch(rows, width)
+        + TensorGather.scratch()
+        + LineGather.scratch(dp_count, 2),
         compiler_params=params(2),
         name="middle_exchange",
-    )(part, x, vec)
+    )(part, x, vec, *weights)
 
 
 def put_rows(base, values):
@@ -484,17 +618,23 @@
     return jnp.sum(value, axis=0, keepdims=True)
 
 
-def back_kernel(part, middle_ref, run_ref, vec_ref, grad_ref, low, sums_ref, *scratch):
-    enter(1)
+def back_kernel(dp_count, *refs):
+    (part, part_out, middle_ref, run_ref, vec_ref, g0, g1,
+     block_out, grad_ref, low, sums_ref, o0, o1, *scratch) = refs
+    enter(dp_count)
     scatter = TensorScatter(part, *scratch[:5])
-    gather = TensorGather(low, *scratch[5:7])
+    scatter_out = TensorScatter(part_out, *scratch[5:10])
+    gather = TensorGather(low, *scratch[10:12])
+    line = LineReduce(dp_count, (g0, g1), (o0, o1), scratch[12:18], *scratch[18:22])
     scatter.start()
+    line.start()
     scatter.middle()
     _, normed, inverse = layer_normalize(middle_ref[...], vec_ref[3:4], vec_ref[4:5])
     upstream = scatter.finish()
     grad = run_ref[...] + norm_backward_step(upstream, vec_ref[3:4], normed, inverse)
     grad_ref[...] = grad
     gather.start(grad.astype(BF16))
+    scatter_out.start()
     sums_ref[...] = put_rows(
         jnp.zeros(sums_ref.shape, F32),
         [
@@ -504,169 +644,81 @@
             (5, column_sum(run_ref[...])),
         ],
     )
+    line.run()
     gather.forward()
+    scatter_out.middle()
+    line.finish()
+    block_out[...] = middle_ref[...] + scatter_out.finish() + vec_ref[5:6]
     gather.finish()
-
-
-def back_exchange(part, middle, run, vec):
+    line.drain()
+
+
+def back_exchange(dp_count, part, part_out, middle, run, vec, grads):
     rows, width = middle.shape
     shape = jax.ShapeDtypeStruct
+    blocks = [g.shape[1:] for g in grads]
     return pl.pallas_call(
-        back_kernel,
+        functools.partial(back_kernel, dp_count),
         out_shape=[
+            shape(middle.shape, F32),
             shape(middle.shape, F32),
             shape((4, rows, width), BF16),
             shape((VECTOR_ROWS, width), F32),
-        ],
-        in_specs=vmem(4),
-        out_specs=vmem(3),
-        scratch_shapes=TensorScatter.scratch(rows, width) + TensorGather.scratch(),
+        ]
+        + [shape(s, F32) for s in blocks],
+        in_specs=vmem(7),
+        out_specs=vmem(6),
+        scratch_shapes=TensorScatter.scratch(rows, width)
+        + TensorScatter.scratch(rows, width)
+        + TensorGather.scratch()
+        + LineReduce.scratch(dp_count, blocks),
         compiler_params=params(3),
         name="back_exchange",
-    )(part, middle, run, vec)
+    )(part, part_out, middle, run, vec, *grads)
 
 
 def reduce_kernel(dp_count, *refs):
-    (part_in, part_out, x_ref, middle_ref, mgrad_ref, vec_ref, sums_ref,
-     g0, g1, g2, g3,
-     block_out, input_grad, sums_out, o0, o1, o2, o3,
-     *scratch) = refs
-    grads, outs = (g0, g1, g2, g3), (o0, o1, o2, o3)
-    held, below, above = scratch[0:4], scratch[4:8], scratch[8:12]
-    xsend, xrecv, zsend, zrecv = scratch[12:16]
-    vsum = VectorSum(dp_count, *scratch[16:22])
-    d, t = place()
-    line, b = d // 2, d % 2
-    line_count = dp_count // 2
+    (part_in, x_ref, mgrad_ref, vec_ref, sums_ref, g0, g1,
+     input_grad, sums_out, o0, o1, *scratch) = refs
     enter(dp_count)
-    scatter_in = TensorScatter(part_in, *scratch[22:27])
-    scatter_out = TensorScatter(part_out, *scratch[27:32])
-
-    def xcopy(w, target):
-        return remote(
-            grads[w].at[target * 2 + (1 - b)], held[w].at[target], xsend.at[w, target],
-            xrecv.at[w, target], line * 2 + (1 - b), t,
-        )
-
-    def zcopy(w, way, target):
-        dst = (below if way == 0 else above)[w]
-        return remote(
-            held[w].at[target], dst.at[target], zsend.at[w, target],
-            zrecv.at[w, way, target], (line + (1 if way == 0 else -1)) * 2 + b, t,
-        )
-
-    def each_target(act):
-        def step(i, carry):
-            @pl.when(line_count - 1 - i > line)
-            def _():
-                act(0, line_count - 1 - i)
-
-            @pl.when(i < line)
-            def _():
-                act(1, i)
-
-            return carry
-
-        lax.fori_loop(0, line_count - 1, step, 0)
-
-    def send_x(way, target):
-        for w in range(4):
-            xcopy(w, target).start()
-
+    line = LineReduce(dp_count, (g0, g1), (o0, o1), scratch[:6], *scratch[6:10])
+    vsum = VectorSum(dp_count, *scratch[10:16])
+    scatter_in = TensorScatter(part_in, *scratch[16:21])
     scatter_in.start()
-    each_target(send_x)
-    send_x(0, line)
+    line.start()
     scatter_in.middle()
-    scatter_out.start()
-    scatter_out.middle()
     _, normed, inverse = layer_normalize(x_ref[...], vec_ref[0:1], vec_ref[1:2])
     upstream = scatter_in.finish()
-    input_grad[...] = mgrad_ref[...] + norm_backward_step(
-        upstream, vec_ref[0:1], normed, inverse
-    )
     vsum.start(
         put_rows(
             sums_ref[...], [(0, column_sum(upstream * normed)), (1, column_sum(upstream))]
         )
     )
-
-    def reduce(way, target):
-        for w in range(4):
-            xcopy(w, target).wait_recv()
-            dst = (below if way == 0 else above)[w]
-            has = (line > 0) if way == 0 else (line + 1 < line_count)
-
-            @pl.when(has)
-            def _():
-                zcopy(w, way, target).wait_recv()
-                held[w][target] = (
-                    grads[w][target * 2 + b].astype(F32)
-                    + held[w][target].astype(F32)
-                    + dst[target].astype(F32)
-                ).astype(BF16)
-
-            @pl.when(jnp.logical_not(has))
-            def _():
-                held[w][target] = (
-                    grads[w][target * 2 + b].astype(F32) + held[w][target].astype(F32)
-                ).astype(BF16)
-
-            zcopy(w, way, target).start()
-
-    each_target(reduce)
-    block_out[...] = middle_ref[...] + scatter_out.finish() + vec_ref[5:6]
+    input_grad[...] = mgrad_ref[...] + norm_backward_step(
+        upstream, vec_ref[0:1], normed, inverse
+    )
+    line.run()
     vsum.middle()
-    for w in range(4):
-        xcopy(w, line).wait_recv()
-        outs[w][...] = grads[w][d].astype(F32) + held[w][line].astype(F32)
-
-        @pl.when(line > 0)
-        def _():
-            zcopy(w, 0, line).wait_recv()
-            outs[w][...] += below[w][line].astype(F32)
-
-        @pl.when(line + 1 < line_count)
-        def _():
-            zcopy(w, 1, line).wait_recv()
-            outs[w][...] += above[w][line].astype(F32)
-
+    line.finish()
     sums_out[...] = vsum.finish()
-
-    def drain(way, target):
-        for w in range(4):
-            zcopy(w, way, target).wait_send()
-            xcopy(w, target).wait_send()
-
-    each_target(drain)
-    for w in range(4):
-        xcopy(w, line).wait_send()
-
-
-def reduce_all(dp_count, part_in, part_out, x, middle, mgrad, vec, sums, grads):
+    line.drain()
+
+
+def reduce_all(dp_count, part_in, x, mgrad, vec, sums, grads):
     rows, width = x.shape
-    line_count = dp_count // 2
     shape = jax.ShapeDtypeStruct
     blocks = [g.shape[1:] for g in grads]
-    lines = [pltpu.VMEM((line_count,) + s, BF16) for s in blocks]
     return pl.pallas_call(
         functools.partial(reduce_kernel, dp_count),
-        out_shape=[shape(x.shape, F32), shape(x.shape, F32), shape(vec.shape, F32)]
-        + [shape(s, F32) for s in blocks],
-        in_specs=vmem(11),
-        out_specs=vmem(7),
-        scratch_shapes=lines * 3
-        + [
-            pltpu.SemaphoreType.DMA((4, line_count)),
-            pltpu.SemaphoreType.DMA((4, line_count)),
-            pltpu.SemaphoreType.DMA((4, line_count)),
-            pltpu.SemaphoreType.DMA((4, 2, line_count)),
-        ]
+        out_shape=[shape(x.shape, F32), shape(vec.shape, F32)] + [shape(s, F32) for s in blocks],
+        in_specs=vmem(7),
+        out_specs=vmem(4),
+        scratch_shapes=LineReduce.scratch(dp_count, blocks)
         + VectorSum.scratch(dp_count, width)
-        + TensorScatter.scratch(rows, width)
         + TensorScatter.scratch(rows, width),
         compiler_params=params(4),
         name="reduce_all",
-    )(part_in, part_out, x, middle, mgrad, vec, sums, *grads)
+    )(part_in, x, mgrad, vec, sums, *grads)
 
 
 def per_device(
@@ -712,18 +764,16 @@
     row_ids = tensor_index * own_rows + jnp.arange(own_rows, dtype=jnp.int32)
     live_rows = (row_ids < group_fill[0]).astype(jnp.float32)[:, None]
     running_gradient = out_grad * live_rows
-    vec, attn_in, out_low, qkv_full, dense_full, up_full, down_full = gather_all(
+    vec, attn_in, out_low, qkv_full, dense_full = gather_all(
         dp_count,
         vec,
         block_input,
         running_gradient.astype(BF16),
-        (qkv_weight, dense_weight, up_weight, down_weight),
+        (qkv_weight, dense_weight),
     )
     attn_in = attn_in.reshape(group_rows, width)
     out_low = out_low.reshape(group_rows, width)
-    qkv_full, dense_full, up_full, down_full = (
-        w.reshape(-1, w.shape[-1]) for w in (qkv_full, dense_full, up_full, down_full)
-    )
+    qkv_full, dense_full = (w.reshape(-1, w.shape[-1]) for w in (qkv_full, dense_full))
     local_heads = qkv_full.shape[1] // (3 * head_dim)
     slopes = head_slopes((tensor_index * local_heads).astype(jnp.float32), local_heads)
     projected = jnp.dot(attn_in, qkv_full, preferred_element_type=jnp.float32).reshape(
@@ -740,9 +790,14 @@
     context, log_total = attention_forward(queries, key_all, values, slopes, seq_begin)
     context_flat = context.reshape(group_rows, local_heads * head_dim)
     attn_part = jnp.dot(context_flat, dense_full, preferred_element_type=jnp.float32).astype(BF16)
-    residual_middle, mlp_in = middle_exchange(
-        attn_part.reshape(4, own_rows, width), block_input, vec
-    )
+    residual_middle, mlp_in, up_full, down_full = middle_exchange(
+        dp_count,
+        attn_part.reshape(4, own_rows, width),
+        block_input,
+        vec,
+        (up_weight, down_weight),
+    )
+    up_full, down_full = (w.reshape(-1, w.shape[-1]) for w in (up_full, down_full))
     mlp_in = mlp_in.reshape(group_rows, width)
     pre_act = jnp.dot(mlp_in, up_full, preferred_element_type=jnp.float32) + vec[6]
     act_value, act_back = jax.vjp(gelu_tanh, pre_act)
@@ -754,16 +809,22 @@
     mlp_in_part = lax.dot_general(
         pre_grad, up_full, CONTRACT_COLS, preferred_element_type=jnp.float32
     ).astype(BF16)
-    residual_middle_gradient, middle_low, sums = back_exchange(
-        mlp_in_part.reshape(4, own_rows, width), residual_middle, running_gradient, vec
-    )
-    middle_low = middle_low.reshape(group_rows, width)
     mlp_part = jnp.dot(activated, down_full, preferred_element_type=jnp.float32).astype(BF16)
     down_grad = lax.dot_general(
         activated, out_low, CONTRACT_ROWS, preferred_element_type=jnp.float32
     )
     up_grad = lax.dot_general(mlp_in, pre_grad, CONTRACT_ROWS, preferred_element_type=jnp.float32)
     up_shift_grad = jnp.sum(pre_grad.astype(jnp.float32), axis=0)
+    block_out, residual_middle_gradient, middle_low, sums, up_out, down_out = back_exchange(
+        dp_count,
+        mlp_in_part.reshape(4, own_rows, width),
+        mlp_part.reshape(4, own_rows, width),
+        residual_middle,
+        running_gradient,
+        vec,
+        tuple(g.astype(BF16).reshape(dp_count, -1, g.shape[-1]) for g in (up_grad, down_grad)),
+    )
+    middle_low = middle_low.reshape(group_rows, width)
     dense_grad = lax.dot_general(
         context_flat, middle_low, CONTRACT_ROWS, preferred_element_type=jnp.float32
     )
@@ -787,14 +848,12 @@
     sums = lax.dynamic_update_slice(sums, qv_grad[None], (7, 0))
     grads = tuple(
         g.astype(BF16).reshape(dp_count, -1, g.shape[-1])
-        for g in (qkv_grad_sum, dense_grad, up_grad, down_grad)
-    )
-    block_out, block_input_gradient, sums, qkv_out, dense_out, up_out, down_out = reduce_all(
+        for g in (qkv_grad_sum, dense_grad)
+    )
+    block_input_gradient, sums, qkv_out, dense_out = reduce_all(
         dp_count,
         attn_in_part.reshape(4, own_rows, width),
-        mlp_part.reshape(4, own_rows, width),
         block_input,
-        residual_middle,
         residual_middle_gradient,
         vec,
         sums,

time: 272 us -> 262 us (0.963)
  Pallas kernels: 208 us -> 199 us
    pallas_call x2, Pallas kernels: 43 us -> 111 us  [the longest x1 58.1 us: back_exchange(): pl.pallas_call(functools.partial(back_kernel, dp_count), out_shape=[shape...]
    pallas_call x1, Pallas kernels: 81.4 us -> 39.6 us  [gather_all(): pl.pallas_call(functools.partial(gather_kernel, dp_count), out_shape=[sha...]
    pallas_call x1, Pallas kernels: 83.7 us -> 48.9 us  [reduce_all(): pl.pallas_call(functools.partial(reduce_kernel, dp_count), out_shape=[sha...]
    unnamed x38 -> x40, local copies, waits for them, and re-layouts: 8.79 us -> 7.66 us
where the time goes in v2:
time: 262 us; the launch traced here: 261 us
  Pallas kernels  199 us (76%)
  matrix products  34.7 us (13%)
  local copies, waits for them, and re-layouts  19.6 us (7%)
  other arithmetic  5.9 us (2%)
    pallas_call x1, Pallas kernels, back_exchange(): pl.pallas_call(functools.partial(back_kernel, dp_count), out_shape=[shape...  58.1 us
    pallas_call x1, Pallas kernels, middle_exchange(): pl.pallas_call(functools.partial(middle_kernel, dp_count), out_shape=[sha...  52.5 us
    pallas_call x1, Pallas kernels, reduce_all(): pl.pallas_call(functools.partial(reduce_kernel, dp_count), out_shape=[sha...  48.9 us
    pallas_call x1, Pallas kernels, gather_all(): pl.pallas_call(functools.partial(gather_kernel, dp_count), out_shape=[sha...  39.6 us
    unnamed x40, local copies, waits for them, and re-layouts  7.66 us

profile of v2, /device:TPU:0, one launch (start us, length us, event | category | flops | bytes accessed | tf_op | source)
XLA Modules:
  0.0 260.8 jit_solution(1144529645006116777)
XLA Ops:
  1.3 0.7 bitcast_convert_fusion
  2.0 0.7 bitcast_convert_fusion.1
  2.6 0.1 pad.6.clone
  2.7 0.8 stack.49
  3.5 0.4 dynamic_update_slice.15
  3.9 0.2 dynamic_update_slice.16
  4.2 0.2 dynamic_update_slice.17.refs_0_
  4.4 0.0 copy-start.10
  4.4 1.5 fusion.13
  6.0 2.0 fusion.17
  8.0 0.1 subtract_convert_fusion
  8.1 0.0 copy-done.10
  8.1 39.6 %gather_all.1 = (f32[8,1024]{1,0:T(8,128)}, bf16[4,128,1024]{2,1,0:T(8,128)(2,1)}, bf16[4,128,1024]{2,1,0:T(8,128)(2,1)}, bf16[8,128,768]{2,1,0:T(8,128)(2,1)}, bf16[8,32,1024]{2,1,0:T(8,128)(2,1)}) custom-call(f32[8,1024]{1,0:T(8,128)} %copy-done.10, f32[128,1024]{1,0:T(8,128)} %refs_1_.5, bf16[128,1024]{1,0:T(8,128)(2,1)} %get-tuple-element.56.refs_2_, ...), custom_call_target="tpu_custom_call" | custom-call | tf_op jit(solution)/shard_map/gather_all/pallas_call | solution.py:556
  47.7 0.7 slice_reduce_fusion
  48.5 0.1 reshape_squeeze.3
  48.6 0.1 pad_maximum_fusion.1
  48.6 0.8 slice.51
  49.4 1.7 copy.43
  51.1 0.0 copy-start.9
  51.1 2.3 add_convert_fusion
  53.4 0.0 copy-done.9
  53.4 1.3 fusion.20
  54.8 0.6 exponential_reduce_fusion
  55.4 1.3 copy-done
  56.7 0.8 convolution_convert_fusion.10
  57.5 0.3 copy-done.4
  57.8 1.5 convolution_convert_fusion.6
  59.2 52.5 %middle_exchange.1 = (f32[128,1024]{1,0:T(8,128)}, bf16[4,128,1024]{2,1,0:T(8,128)(2,1)}, bf16[8,128,1024]{2,1,0:T(8,128)(2,1)}, bf16[8,128,1024]{2,1,0:T(8,128)(2,1)}) custom-call(bf16[4,128,1024]{2,1,0:T(8,128)(2,1)} %bitcast.118, f32[128,1024]{1,0:T(8,128)} %refs_1_.5, f32[8,1024]{1,0:T(8,128)} %get-tuple-element.36.refs_2_.refs_4_.refs_3_, ...), custom_call_target="tpu_custom_call" | custom-call | tf_op jit(solution)/shard_map/middle_exchange/pallas_call | solution.py:596
  111.7 0.0 copy-start.13
  111.7 3.3 %fusion.21 = f32[512,1024]{1,0:T(8,128)S(1)} fusion(bf16[512,1024]{1,0:T(8,128)(2,1)} %bitcast.158, bf16[1024,1024]{1,0:T(8,128)(2,1)} %bitcast.150), kind=kOutput, calls=%fused_computation.67 | convolution fusion | flops 1073741824 | bytes 5242880 | tf_op jit(solution)/shard_map/dot_general | solution.py:802
  115.1 2.5 convolution_convert_fusion.4
  117.6 2.5 convert_reduce_fusion
  120.1 3.0 %convolution_convert_fusion = bf16[1024,1024]{1,0:T(8,128)(2,1)} fusion(bf16[512,1024]{1,0:T(8,128)(2,1)S(1)} %bitcast.157, f32[512,1024]{1,0:T(8,128)S(1)} %fusion.21, f32[1024]{0:T(1024)S(1)} %bitcast.143), kind=kOutput, calls=%fused_computation.16 | convolution fusion | flops 1080033280 | bytes 5246976 | tf_op jit(solution)/shard_map/dot_general | solution.py:813
  123.1 2.3 convolution_convert_fusion.5
  125.4 2.6 %convolution_convert_fusion.1 = bf16[1024,1024]{1,0:T(8,128)(2,1)} fusion(bf16[512,1024]{1,0:T(8,128)(2,1)S(1)} %bitcast.159, bf16[512,1024]{1,0:T(8,128)(2,1)S(1)} %get-tuple-element.55), kind=kOutput, calls=%fused_computation.17 | convolution fusion | flops 1074790400 | bytes 4194304 | tf_op jit(solution)/shard_map/dot_general | solution.py:816
  128.0 58.1 %back_exchange.1 = (f32[128,1024]{1,0:T(8,128)}, f32[128,1024]{1,0:T(8,128)}, bf16[4,128,1024]{2,1,0:T(8,128)(2,1)}, f32[8,1024]{1,0:T(8,128)}, f32[128,1024]{1,0:T(8,128)}, /*index=5*/f32[128,1024]{1,0:T(8,128)}) custom-call(bf16[4,128,1024]{2,1,0:T(8,128)(2,1)} %bitcast.129, bf16[4,128,1024]{2,1,0:T(8,128)(2,1)} %bitcast.128, ...), custom_call_target="tpu_custom_call" | custom-call | tf_op jit(solution)/shard_map/back_exchange/pallas_call | solution.py:660
  186.1 0.0 copy-start.3
  186.1 1.8 multiply_reduce_fusion
  187.9 1.2 convolution_convert_fusion.7
  189.2 1.4 dynamic_update_slice.18
  190.6 3.1 %fusion.12 = bf16[512,4,1,64]{0,3,1,2:T(8,128)(2,1)S(1)} fusion(bf16[512,4,64]{0,2,1:T(8,128)(2,1)S(1)} %bitcast.133, f32[4,512,512]{1,2,0:T(8,128)} %copy-done, f32[4,512]{1,0:T(4,128)S(1)} %log_add_fusion), kind=kOutput, calls=%fused_computation.35 | convolution fusion | flops 136445952 | bytes 4726784 | tf_op jit(solution)/shard_map/hqk,qhd->khd/dot_general | solution.py:81
  193.7 0.3 copy-done.1
  194.0 1.0 multiply_convert_fusion
  195.0 0.8 fusion.10
  195.8 0.5 fusion.11
  196.3 0.2 convert_reduce_fusion.1
  196.5 0.1 broadcast_in_dim_reshape.3
  196.6 1.5 dynamic_update_slice.19.refs_4_
  198.1 0.1 copy.49
  198.2 0.0 copy-done.2
  198.2 0.0 copy-start.14
  198.2 2.0 convolution_convert_fusion.3
  200.2 2.2 convolution_convert_fusion.2
  202.4 48.9 %reduce_all.1 = (f32[128,1024]{1,0:T(8,128)}, f32[8,1024]{1,0:T(8,128)}, f32[128,768]{1,0:T(8,128)}, f32[32,1024]{1,0:T(8,128)}) custom-call(bf16[4,128,1024]{2,1,0:T(8,128)(2,1)} %bitcast.132, f32[128,1024]{1,0:T(8,128)} %refs_1_.5, f32[128,1024]{1,0:T(8,128)} %get-tuple-element.44.refs_2_, f32[8,1024]{1,0:T(8,128)} %get-tuple-element.36.refs_2_.refs_4_.refs_3_, ...), custom_call_target="tpu_custom_call" | custom-call | tf_op jit(solution)/shard_map/reduce_all/pallas_call | solution.py:711
  251.3 1.3 dynamic-slice_bitcast_fusion
  252.6 1.3 dynamic-slice_bitcast_fusion.1
  253.9 0.7 constant_dynamic-slice_fusion
  254.6 0.5 slice_bitcast_fusion.9
  255.2 0.8 copy.69
  256.0 1.9 copy.70
  257.9 0.7 copy.71
  258.6 0.7 copy.72
  259.3 0.8 copy.73
  260.1 0.8 copy.74
  (31 shorter events, 0.1 us)
Async XLA Ops:
  4.4 3.7 %copy-start.10 = (f32[8,1024]{1,0:T(8,128)}, f32[8,1024]{1,0:T(8,128)S(1)}, u32[]{:S(2)}) copy-start(f32[8,1024]{1,0:T(8,128)S(1)} %dynamic_update_slice.17.refs_0_) | copy-start | bytes 98308
  51.1 2.3 copy-start.9
  54.8 2.0 copy-start
  56.7 1.0 copy-start.4
  111.7 3.3 %copy-start.13 = (bf16[8,128,1024]{2,1,0:T(8,128)(2,1)S(1)}, bf16[8,128,1024]{2,1,0:T(8,128)(2,1)}, u32[]{:S(2)}) copy-start(bf16[8,128,1024]{2,1,0:T(8,128)(2,1)} %get-tuple-element.38) | copy-start | bytes 6291460
  115.1 2.6 copy-start.15
  120.1 3.0 %copy-start.12 = (bf16[8,128,1024]{2,1,0:T(8,128)(2,1)S(1)}, bf16[8,128,1024]{2,1,0:T(8,128)(2,1)}, u32[]{:S(2)}) copy-start(bf16[8,128,1024]{2,1,0:T(8,128)(2,1)} %get-tuple-element.40) | copy-start | bytes 6291460
  123.1 2.3 copy-start.16
  186.1 1.8 copy-start.3
  190.6 3.4 %copy-start.1 = (f32[4,512,512]{1,2,0:T(8,128)S(1)}, f32[4,512,512]{1,2,0:T(8,128)}, u32[]{:S(2)}) copy-start(f32[4,512,512]{1,2,0:T(8,128)} %copy-done) | copy-start | bytes 12582916
  196.3 1.9 copy-start.2
  198.2 2.0 copy-start.14
  202.4 52.8 %copy-start.7 = (f32[128,1024]{1,0:T(8,128)S(1)}, f32[128,1024]{1,0:T(8,128)}, u32[]{:S(2)}) copy-start(f32[128,1024]{1,0:T(8,128)} %get-tuple-element.86) | copy-start | bytes 1572868
  251.3 6.6 %copy-start.8 = (f32[128,768]{1,0:T(8,128)S(1)}, f32[128,768]{1,0:T(8,128)}, u32[]{:S(2)}) copy-start(f32[128,768]{1,0:T(8,128)} %get-tuple-element.90) | copy-start | bytes 1179652
  251.3 7.3 %copy-start.11 = (f32[32,1024]{1,0:T(8,128)S(1)}, f32[32,1024]{1,0:T(8,128)}, u32[]{:S(2)}) copy-start(f32[32,1024]{1,0:T(8,128)} %get-tuple-element.92) | copy-start | bytes 393220
  251.3 8.0 %copy-start.6 = (f32[128,1024]{1,0:T(8,128)S(1)}, f32[128,1024]{1,0:T(8,128)}, u32[]{:S(2)}) copy-start(f32[128,1024]{1,0:T(8,128)} %get-tuple-element.96) | copy-start | bytes 1572868
  255.2 4.9 %copy-start.5 = (f32[128,1024]{1,0:T(8,128)S(1)}, f32[128,1024]{1,0:T(8,128)}, u32[]{:S(2)}) copy-start(f32[128,1024]{1,0:T(8,128)} %get-tuple-element.98) | copy-start | bytes 1572868

commit v3 on v2

--- a/solution.py
+++ b/solution.py
@@ -348,7 +348,7 @@
             self.xcopy(w, self.line, self.b, own).start()
             self.local(w).start()
 
-    def hops(self, act, sending=False):
+    def hops(self, act, first, last, sending=False):
         def hop(step, carry):
             for w in range(len(self.weights)):
                 for way in range(2):
@@ -364,9 +364,12 @@
 
             return carry
 
-        lax.fori_loop(1, self.line_count, hop, 0)
-
-    def relay(self):
+        if first < last:
+            lax.fori_loop(first, last, hop, 0)
+
+    def relay(self, first=1, last=None):
+        last = self.line_count if last is None else min(last, self.line_count)
+
         def act(w, way, step, blk, src):
             self.zcopy(w, way, step, blk, src).wait_recv()
 
@@ -376,7 +379,7 @@
 
             self.xcopy(w, blk, self.b, src).start()
 
-        self.hops(act)
+        self.hops(act, first, last)
 
     def finish(self):
         for w in range(len(self.weights)):
@@ -390,7 +393,7 @@
         def act(w, way, step, blk, src):
             self.zcopy(w, way, step, blk, src).wait_send()
 
-        self.hops(act, sending=True)
+        self.hops(act, 1, self.line_count, sending=True)
 
         def pair(blk, carry):
             for w in range(len(self.weights)):
@@ -437,8 +440,9 @@
             (self.line + (1 if way == 0 else -1)) * 2 + self.b, self.t,
         )
 
-    def each_target(self, act):
+    def each_target(self, act, first=0, stop=None):
         last = self.line_count - 1
+        stop = last if stop is None else min(stop, last)
 
         def step(i, carry):
             @pl.when(last - i > self.line)
@@ -451,7 +455,8 @@
 
             return carry
 
-        lax.fori_loop(0, last, step, 0)
+        if first < stop:
+            lax.fori_loop(first, stop, step, 0)
 
     def start(self):
         def send(way, target):
@@ -464,7 +469,7 @@
     def has(self, way):
         return (self.line > 0) if way == 0 else (self.line + 1 < self.line_count)
 
-    def run(self):
+    def run(self, first=0, stop=None):
         def reduce(way, target):
             for w in range(self.n):
                 self.xcopy(w, target).wait_recv()
@@ -488,7 +493,7 @@
 
                 self.zcopy(w, way, target).start()
 
-        self.each_target(reduce)
+        self.each_target(reduce, first, stop)
 
     def finish(self):
         for w in range(self.n):
@@ -524,11 +529,12 @@
     weights.start()
     gather_o.start(og_ref[...])
     vsum.middle()
+    weights.relay(1, 2)
     vec = vsum.finish()
     vec_out[...] = vec
     normed = layer_normalize(x_ref[...], vec[0:1], vec[1:2])[0]
     gather_x.start(normed.astype(BF16))
-    weights.relay()
+    weights.relay(2)
     gather_o.forward()
     gather_x.forward()
     weights.finish()
@@ -629,6 +635,7 @@
     scatter.start()
     line.start()
     scatter.middle()
+    line.run(0, 1)
     _, normed, inverse = layer_normalize(middle_ref[...], vec_ref[3:4], vec_ref[4:5])
     upstream = scatter.finish()
     grad = run_ref[...] + norm_backward_step(upstream, vec_ref[3:4], normed, inverse)
@@ -644,9 +651,10 @@
             (5, column_sum(run_ref[...])),
         ],
     )
-    line.run()
+    line.run(1, 2)
     gather.forward()
     scatter_out.middle()
+    line.run(2)
     line.finish()
     block_out[...] = middle_ref[...] + scatter_out.finish() + vec_ref[5:6]
     gather.finish()
@@ -687,6 +695,7 @@
     scatter_in.start()
     line.start()
     scatter_in.middle()
+    line.run(0, 1)
     _, normed, inverse = layer_normalize(x_ref[...], vec_ref[0:1], vec_ref[1:2])
     upstream = scatter_in.finish()
     vsum.start(
@@ -697,8 +706,9 @@
     input_grad[...] = mgrad_ref[...] + norm_backward_step(
         upstream, vec_ref[0:1], normed, inverse
     )
-    line.run()
+    line.run(1, 2)
     vsum.middle()
+    line.run(2)
     line.finish()
     sums_out[...] = vsum.finish()
     line.drain()

time: 262 us -> 254 us (0.969)
  Pallas kernels: 199 us -> 192 us
    pallas_call x1, Pallas kernels: 58.1 us -> 53.8 us  [back_exchange(): pl.pallas_call(functools.partial(back_kernel, dp_count), out_shape=[shape...]
where the time goes in v3:
time: 254 us
  Pallas kernels  192 us (76%)
  matrix products  34.7 us (14%)
  local copies, waits for them, and re-layouts  19.6 us (8%)
  other arithmetic  5.9 us (2%)
    pallas_call x1, Pallas kernels, back_exchange(): pl.pallas_call(functools.partial(back_kernel, dp_count), out_shape=[shape...  53.8 us
    pallas_call x1, Pallas kernels, middle_exchange(): pl.pallas_call(functools.partial(middle_kernel, dp_count), out_shape=[sha...  51.9 us
    pallas_call x1, Pallas kernels, reduce_all(): pl.pallas_call(functools.partial(reduce_kernel, dp_count), out_shape=[sha...  47.1 us
    pallas_call x1, Pallas kernels, gather_all(): pl.pallas_call(functools.partial(gather_kernel, dp_count), out_shape=[sha...  38.9 us
    unnamed x40, local copies, waits for them, and re-layouts  7.66 us

profile of v3, /device:TPU:0, one launch (start us, length us, event | category | flops | bytes accessed | tf_op | source)
XLA Modules:
  0.0 253.6 jit_solution(14217016479928054582)
XLA Ops:
  1.3 0.7 bitcast_convert_fusion
  2.0 0.7 bitcast_convert_fusion.1
  2.6 0.1 pad.6.clone
  2.7 0.8 stack.49
  3.5 0.4 dynamic_update_slice.15
  3.9 0.2 dynamic_update_slice.16
  4.2 0.2 dynamic_update_slice.17.refs_0_
  4.4 0.0 copy-start.10
  4.4 1.5 fusion.13
  6.0 2.0 fusion.17
  8.0 0.1 subtract_convert_fusion
  8.1 38.9 %gather_all.1 = (f32[8,1024]{1,0:T(8,128)}, bf16[4,128,1024]{2,1,0:T(8,128)(2,1)}, bf16[4,128,1024]{2,1,0:T(8,128)(2,1)}, bf16[8,128,768]{2,1,0:T(8,128)(2,1)}, bf16[8,32,1024]{2,1,0:T(8,128)(2,1)}) custom-call(f32[8,1024]{1,0:T(8,128)} %copy-done.10, f32[128,1024]{1,0:T(8,128)} %refs_1_.5, bf16[128,1024]{1,0:T(8,128)(2,1)} %get-tuple-element.56.refs_2_, ...), custom_call_target="tpu_custom_call" | custom-call | tf_op jit(solution)/shard_map/gather_all/pallas_call | solution.py:562
  47.0 0.7 slice_reduce_fusion
  47.8 0.1 reshape_squeeze.3
  47.9 0.1 pad_maximum_fusion.1
  48.0 0.8 slice.51
  48.7 1.7 copy.43
  50.4 0.0 copy-start.9
  50.4 2.3 add_convert_fusion
  52.7 0.0 copy-done.9
  52.7 1.3 fusion.20
  54.1 0.0 copy-start
  54.1 0.6 exponential_reduce_fusion
  54.7 1.3 copy-done
  56.0 0.8 convolution_convert_fusion.10
  56.8 0.3 copy-done.4
  57.1 1.5 convolution_convert_fusion.6
  58.5 51.9 %middle_exchange.1 = (f32[128,1024]{1,0:T(8,128)}, bf16[4,128,1024]{2,1,0:T(8,128)(2,1)}, bf16[8,128,1024]{2,1,0:T(8,128)(2,1)}, bf16[8,128,1024]{2,1,0:T(8,128)(2,1)}) custom-call(bf16[4,128,1024]{2,1,0:T(8,128)(2,1)} %bitcast.118, f32[128,1024]{1,0:T(8,128)} %refs_1_.5, f32[8,1024]{1,0:T(8,128)} %get-tuple-element.36.refs_2_.refs_4_.refs_3_, ...), custom_call_target="tpu_custom_call" | custom-call | tf_op jit(solution)/shard_map/middle_exchange/pallas_call | solution.py:602
  110.5 3.3 %fusion.21 = f32[512,1024]{1,0:T(8,128)S(1)} fusion(bf16[512,1024]{1,0:T(8,128)(2,1)} %bitcast.158, bf16[1024,1024]{1,0:T(8,128)(2,1)} %bitcast.150), kind=kOutput, calls=%fused_computation.67 | convolution fusion | flops 1073741824 | bytes 5242880 | tf_op jit(solution)/shard_map/dot_general | solution.py:812
  113.8 2.6 %convolution_convert_fusion.4 = bf16[512,1024]{1,0:T(8,128)(2,1)} fusion(bf16[1024,1024]{1,0:T(8,128)(2,1)S(1)} %bitcast.152, f32[512,1024]{1,0:T(8,128)S(1)} %fusion.21, f32[1024]{0:T(1024)S(1)} %bitcast.141), kind=kOutput, calls=%fused_computation.22 | convolution fusion | flops 1079508992 | bytes 5246976 | tf_op jit(solution)/shard_map/dot_general | solution.py:822
  116.4 2.5 convert_reduce_fusion
  118.9 3.0 %convolution_convert_fusion = bf16[1024,1024]{1,0:T(8,128)(2,1)} fusion(bf16[512,1024]{1,0:T(8,128)(2,1)S(1)} %bitcast.157, f32[512,1024]{1,0:T(8,128)S(1)} %fusion.21, f32[1024]{0:T(1024)S(1)} %bitcast.143), kind=kOutput, calls=%fused_computation.16 | convolution fusion | flops 1080033280 | bytes 5246976 | tf_op jit(solution)/shard_map/dot_general | solution.py:823
  121.9 2.3 convolution_convert_fusion.5
  124.2 0.0 copy-done.16
  124.2 2.6 %convolution_convert_fusion.1 = bf16[1024,1024]{1,0:T(8,128)(2,1)} fusion(bf16[512,1024]{1,0:T(8,128)(2,1)S(1)} %bitcast.159, bf16[512,1024]{1,0:T(8,128)(2,1)S(1)} %get-tuple-element.55), kind=kOutput, calls=%fused_computation.17 | convolution fusion | flops 1074790400 | bytes 4194304 | tf_op jit(solution)/shard_map/dot_general | solution.py:826
  126.8 53.8 %back_exchange.1 = (f32[128,1024]{1,0:T(8,128)}, f32[128,1024]{1,0:T(8,128)}, bf16[4,128,1024]{2,1,0:T(8,128)(2,1)}, f32[8,1024]{1,0:T(8,128)}, f32[128,1024]{1,0:T(8,128)}, /*index=5*/f32[128,1024]{1,0:T(8,128)}) custom-call(bf16[4,128,1024]{2,1,0:T(8,128)(2,1)} %bitcast.129, bf16[4,128,1024]{2,1,0:T(8,128)(2,1)} %bitcast.128, ...), custom_call_target="tpu_custom_call" | custom-call | tf_op jit(solution)/shard_map/back_exchange/pallas_call | solution.py:668
  180.6 0.0 copy-start.3
  180.6 1.8 multiply_reduce_fusion
  182.4 1.2 convolution_convert_fusion.7
  183.6 1.4 dynamic_update_slice.18
  185.0 3.1 %fusion.12 = bf16[512,4,1,64]{0,3,1,2:T(8,128)(2,1)S(1)} fusion(bf16[512,4,64]{0,2,1:T(8,128)(2,1)S(1)} %bitcast.133, f32[4,512,512]{1,2,0:T(8,128)} %copy-done, f32[4,512]{1,0:T(4,128)S(1)} %log_add_fusion), kind=kOutput, calls=%fused_computation.35 | convolution fusion | flops 136445952 | bytes 4726784 | tf_op jit(solution)/shard_map/hqk,qhd->khd/dot_general | solution.py:81
  188.1 0.3 copy-done.1
  188.5 1.0 multiply_convert_fusion
  189.5 0.8 fusion.10
  190.3 0.5 fusion.11
  190.7 0.0 copy-start.2
  190.8 0.2 convert_reduce_fusion.1
  191.0 0.1 broadcast_in_dim_reshape.3
  191.1 1.5 dynamic_update_slice.19.refs_4_
  192.6 0.1 copy.49
  192.7 2.0 convolution_convert_fusion.3
  194.7 0.0 copy-done.14
  194.7 2.2 convolution_convert_fusion.2
  196.9 47.1 %reduce_all.1 = (f32[128,1024]{1,0:T(8,128)}, f32[8,1024]{1,0:T(8,128)}, f32[128,768]{1,0:T(8,128)}, f32[32,1024]{1,0:T(8,128)}) custom-call(bf16[4,128,1024]{2,1,0:T(8,128)(2,1)} %bitcast.132, f32[128,1024]{1,0:T(8,128)} %refs_1_.5, f32[128,1024]{1,0:T(8,128)} %get-tuple-element.44.refs_2_, f32[8,1024]{1,0:T(8,128)} %get-tuple-element.36.refs_2_.refs_4_.refs_3_, ...), custom_call_target="tpu_custom_call" | custom-call | tf_op jit(solution)/shard_map/reduce_all/pallas_call | solution.py:721
  244.0 1.3 dynamic-slice_bitcast_fusion
  245.4 1.3 dynamic-slice_bitcast_fusion.1
  246.6 0.7 constant_dynamic-slice_fusion
  247.4 0.5 slice_bitcast_fusion.9
  247.9 0.8 copy.69
  248.7 1.9 copy.70
  250.6 0.7 copy.71
  251.3 0.7 copy.72
  252.0 0.8 copy.73
  252.8 0.8 copy.74
  (31 shorter events, 0.1 us)
Async XLA Ops:
  4.4 3.7 %copy-start.10 = (f32[8,1024]{1,0:T(8,128)}, f32[8,1024]{1,0:T(8,128)S(1)}, u32[]{:S(2)}) copy-start(f32[8,1024]{1,0:T(8,128)S(1)} %dynamic_update_slice.17.refs_0_) | copy-start | bytes 98308
  50.4 2.3 copy-start.9
  54.1 2.0 copy-start
  56.0 1.0 copy-start.4
  110.5 3.3 %copy-start.13 = (bf16[8,128,1024]{2,1,0:T(8,128)(2,1)S(1)}, bf16[8,128,1024]{2,1,0:T(8,128)(2,1)}, u32[]{:S(2)}) copy-start(bf16[8,128,1024]{2,1,0:T(8,128)(2,1)} %get-tuple-element.38) | copy-start | bytes 6291460
  113.8 2.6 %copy-start.15 = (bf16[4,128,1024]{2,1,0:T(8,128)(2,1)S(1)}, bf16[4,128,1024]{2,1,0:T(8,128)(2,1)}, u32[]{:S(2)}) copy-start(bf16[4,128,1024]{2,1,0:T(8,128)(2,1)} %get-tuple-element.33) | copy-start | bytes 3145732
  118.9 3.0 %copy-start.12 = (bf16[8,128,1024]{2,1,0:T(8,128)(2,1)S(1)}, bf16[8,128,1024]{2,1,0:T(8,128)(2,1)}, u32[]{:S(2)}) copy-start(bf16[8,128,1024]{2,1,0:T(8,128)(2,1)} %get-tuple-element.40) | copy-start | bytes 6291460
  121.9 2.3 copy-start.16
  180.6 1.8 copy-start.3
  185.0 3.4 %copy-start.1 = (f32[4,512,512]{1,2,0:T(8,128)S(1)}, f32[4,512,512]{1,2,0:T(8,128)}, u32[]{:S(2)}) copy-start(f32[4,512,512]{1,2,0:T(8,128)} %copy-done) | copy-start | bytes 12582916
  190.7 1.9 copy-start.2
  192.6 2.0 copy-start.14
  196.9 51.0 %copy-start.7 = (f32[128,1024]{1,0:T(8,128)S(1)}, f32[128,1024]{1,0:T(8,128)}, u32[]{:S(2)}) copy-start(f32[128,1024]{1,0:T(8,128)} %get-tuple-element.86) | copy-start | bytes 1572868
  244.0 6.6 %copy-start.8 = (f32[128,768]{1,0:T(8,128)S(1)}, f32[128,768]{1,0:T(8,128)}, u32[]{:S(2)}) copy-start(f32[128,768]{1,0:T(8,128)} %get-tuple-element.90) | copy-start | bytes 1179652
  244.0 7.3 %copy-start.11 = (f32[32,1024]{1,0:T(8,128)S(1)}, f32[32,1024]{1,0:T(8,128)}, u32[]{:S(2)}) copy-start(f32[32,1024]{1,0:T(8,128)} %get-tuple-element.92) | copy-start | bytes 393220
  244.0 8.0 %copy-start.6 = (f32[128,1024]{1,0:T(8,128)S(1)}, f32[128,1024]{1,0:T(8,128)}, u32[]{:S(2)}) copy-start(f32[128,1024]{1,0:T(8,128)} %get-tuple-element.96) | copy-start | bytes 1572868
  247.9 4.9 %copy-start.5 = (f32[128,1024]{1,0:T(8,128)S(1)}, f32[128,1024]{1,0:T(8,128)}, u32[]{:S(2)}) copy-start(f32[128,1024]{1,0:T(8,128)} %get-tuple-element.98) | copy-start | bytes 1572868
